TPU v7x, 256 devices: a whole 4x4x8 slice. The times are simulated.
256 devices in a mesh: row: 16 (over y, x), col: 16 (over z, core).
Axes of the slice: x: 4, y: 4, z: 8, core: 2. Of those that a mesh axis runs over, the one named last changes fastest.
Arguments:
- rhs: float32 [128, 32768], P('row', 'col'), may hold values from -60 to 60
- flex_tiles: float32 [131072, 2048], P('row', 'col'), may hold values from -0.25 to 0.25
- flex_cols: int32 [256, 64], P('row', 'col'), may hold values from 0 to 15, as said below
- stiff_tiles: float32 [131072, 2048], P('row', 'col'), may hold values from -0.25 to 0.25
- stiff_cols: int32 [256, 64], P('row', 'col'), may hold values from 0 to 15, as said below
- deflation: float32 [512, 32768], P('row', 'col'), may hold values from -0.375 to 0.375
- coarse_rows: float32 [8192, 8192], P(('row', 'col')), may hold values from -5 to 5, as said below
- face_rows: int32 [64, 2048], P('row', 'col'), may hold values from 0 to 2047, as said below
- face_len: int32 [16, 64], P('row', 'col'), may hold values from 0 to 128, as said below
Outputs:
- solution: float32 [128, 32768], P('row', 'col')
- residual: float32 [128, 32768], P('row', 'col')
- correction: float32 [128, 32768], P('row', 'col')
Inputs may be any that keep to these rules, and one draw needn't show every extreme that they name: `flex_cols`: row b of a subdomain's block list names 4 different block columns, the first being b. `stiff_cols`: row b of a subdomain's block list names 4 different block columns, the first being b. `coarse_rows`: the whole matrix is symmetric. `face_rows`: the four lists of a subdomain name 512 different multipliers of it. `face_len`: the two subdomains of a face give it the same length; faces on the grid's boundary have length 0, inner faces at least 32.
All inputs are finite; a program needn't handle non-finite values.
Results may differ from a plain program's by a relative error of at most 0.0003.
Values sent between devices are 32-bit elements; how exact they have to be, the bound alone decides.
A program may use at most 64 MiB of HBM per device.

v0:
```python
import jax
import jax.numpy as jnp
from jax import lax
from jax.sharding import PartitionSpec as P

ITERS = 3


PRECISE = lax.Precision.HIGHEST


def with_halo(cells, sides, width):
    for axis, dim in sides:
        count = lax.axis_size(axis)
        ends = count - 1
        head = lax.slice_in_dim(cells, 0, width, axis=dim)
        tail = lax.slice_in_dim(cells, cells.shape[dim] - width, cells.shape[dim], axis=dim)
        cells = jnp.concatenate(
            [
                lax.ppermute(tail, axis, [(i, (i + 1) % count) for i in range(ends)]),
                cells,
                lax.ppermute(head, axis, [((i + 1) % count, i) for i in range(ends)]),
            ],
            axis=dim,
        )
    return cells


def sparse_forward(vector, tile_set, columns):
    load_count = vector.shape[0]
    blocks, per_row = columns.shape
    tile_width = tile_set.shape[-1]
    pieces = vector.reshape(load_count, blocks, tile_width)
    picked = jnp.take(pieces, columns.reshape(-1), axis=1).reshape(
        load_count, blocks, per_row, tile_width
    )
    product = jnp.einsum("lbkw,bkwv->lbv", picked, tile_set, precision=PRECISE)
    return product.reshape(load_count, blocks * tile_width)


def sparse_backward(vector, tile_set, columns):
    load_count = vector.shape[0]
    blocks, per_row = columns.shape
    tile_width = tile_set.shape[-1]
    pieces = vector.reshape(load_count, blocks, tile_width)
    product = jnp.einsum("lbv,bkwv->lbkw", pieces, tile_set, precision=PRECISE)
    onehot = (columns[:, :, None] == jnp.arange(blocks, dtype=jnp.int32)[None, None, :]).astype(
        jnp.float32
    )
    summed = jnp.einsum("lbkw,bkj->ljw", product, onehot, precision=PRECISE)
    return summed.reshape(load_count, blocks * tile_width)


def pair_totals(first_field, second_field, third_field, fourth_field):
    return lax.psum(
        (jnp.sum(first_field * second_field, axis=1), jnp.sum(third_field * fourth_field, axis=1)),
        ("row", "col"),
    )


def shards(
    rhs, flex_tiles, flex_cols, stiff_tiles, stiff_cols, deflation, coarse_rows, face_rows, face_len
):
    blocks, per_row = flex_cols.shape
    tile_width = flex_tiles.shape[1]
    flex_set = flex_tiles.reshape(blocks, per_row, tile_width, tile_width)
    stiff_set = stiff_tiles.reshape(blocks, per_row, tile_width, tile_width)
    face_width = face_rows.shape[1]
    flat_index = face_rows.reshape(-1)
    slots = jnp.arange(face_width, dtype=jnp.int32)
    live_mask = (slots[None, :] < face_len.reshape(4, 1)).astype(jnp.float32)

    def face_part(vector):
        load_count = vector.shape[0]
        traces = jnp.take(vector, flat_index, axis=1).reshape(load_count, 4, face_width)
        across_rows = with_halo(traces[:, 0:2], (("row", 1),), 1)
        across_cols = with_halo(traces[:, 2:4], (("col", 1),), 1)
        partner = jnp.stack(
            [across_rows[:, 0], across_rows[:, 3], across_cols[:, 0], across_cols[:, 3]], axis=1
        )
        jump_values = (traces - partner) * live_mask[None]
        return (
            jnp.zeros_like(vector)
            .at[:, flat_index]
            .add(jump_values.reshape(load_count, 4 * face_width))
        )

    def operate(vector):
        coupling = face_part(vector)
        after_flex = sparse_forward(vector, flex_set, flex_cols)
        after_stiff = sparse_forward(after_flex, stiff_set, stiff_cols)
        back_stiff = sparse_backward(after_stiff, stiff_set, stiff_cols)
        local_part = sparse_backward(back_stiff, flex_set, flex_cols)
        return vector + local_part + coupling

    def precondition(vector):
        coefficients = jnp.einsum("lm,dm->ld", vector, deflation, precision=PRECISE)
        energy = jnp.einsum(
            "ln,dn->ld",
            lax.all_gather(coefficients, ("row", "col"), axis=1, tiled=True),
            coarse_rows,
            precision=PRECISE,
        )
        return vector + jnp.einsum("ld,dm->lm", energy, deflation, precision=PRECISE)

    residual = rhs
    solution = jnp.zeros_like(rhs)
    correction = precondition(residual)
    direction = correction
    image = operate(direction)
    curvature_sum, descent_sum = pair_totals(direction, image, residual, direction)
    for iteration in range(ITERS):
        step_size = (descent_sum / curvature_sum)[:, None]
        solution = solution + step_size * direction
        residual = residual - step_size * image
        correction = precondition(residual)
        if iteration + 1 < ITERS:
            cross_sum = lax.psum(jnp.sum(correction * image, axis=1), ("row", "col"))
            blend = -cross_sum / curvature_sum
            direction = correction + blend[:, None] * direction
            image = operate(direction)
            curvature_sum, descent_sum = pair_totals(direction, image, residual, direction)
    return (solution, residual, correction)


def solution(mesh):
    return jax.shard_map(
        shards,
        mesh=mesh,
        in_specs=(
            P("row", "col"),
            P("row", "col"),
            P("row", "col"),
            P("row", "col"),
            P("row", "col"),
            P("row", "col"),
            P(("row", "col"), None),
            P("row", "col"),
            P("row", "col"),
        ),
        out_specs=(P("row", "col"), P("row", "col"), P("row", "col")),
        check_vma=False,
    )
```

profile of v0, /device:TPU:1, one launch (start us, length us, event | category | flops | bytes accessed | tf_op | source)
XLA Modules:
  0.0 747.8 jit_solution(5366016694959184341)
XLA Ops:
  3.4 67.8 %all-gather = f32[256,32,8]{1,2,0:T(8,128)S(1)} all-gather(f32[1,32,8]{1,2,0:T(8,128)S(1)} %convolution_bitcast_fusion.21), channel_id=1, replica_groups=mesh['row'=16,'col'=16] {'row','col'}, dimensions={0}, use_global_device_ids=true | all-gather | bytes 263168 | tf_op jit(solution)/shard_map/all_gather | solution.py:100
  84.8 3.8 convolution_bitcast_fusion.17
  89.4 4.0 convolution_bitcast_fusion.16
  93.5 3.6 convolution_bitcast_fusion.5
  97.4 3.6 convolution_bitcast_fusion.4
  102.2 4.2 scatter_custom_fusion
  106.9 78.0 %all-reduce.2 = (f32[8]{0:T(128)S(1)}, f32[8]{0:T(128)S(1)}) all-reduce(f32[8]{0:T(128)S(1)} %get-tuple-element.10, f32[8]{0:T(128)S(1)} %get-tuple-element.9), channel_id=1, replica_groups=mesh['row'=16,'col'=16] {'row','col'}, use_global_device_ids=true, to_apply=%region_1.2 | all-reduce | flops 16 | bytes 128 | tf_op jit(solution)/shard_map/psum | solution.py:55
  185.2 60.6 %all-gather.1 = f32[256,32,8]{1,2,0:T(8,128)S(1)} all-gather(f32[1,32,8]{1,2,0:T(8,128)S(1)} %convolution_bitcast_fusion.20), channel_id=1, replica_groups=mesh['row'=16,'col'=16] {'row','col'}, dimensions={0}, use_global_device_ids=true | all-gather | bytes 263168 | tf_op jit(solution)/shard_map/all_gather | solution.py:100
  247.8 75.0 %psum.58 = f32[8]{0:T(128)S(1)} all-reduce(f32[8]{0:T(128)S(1)} %get-tuple-element.31), channel_id=1, replica_groups=mesh['row'=16,'col'=16] {'row','col'}, use_global_device_ids=true, to_apply=%region_6.9 | all-reduce | flops 8 | bytes 64 | tf_op jit(solution)/shard_map/psum | solution.py:118
  327.5 4.5 collective-permute-start.6
  335.0 3.8 convolution_bitcast_fusion.15
  339.7 4.0 convolution_bitcast_fusion.14
  347.6 3.6 convolution_bitcast_fusion.2
  352.4 3.9 scatter_custom_fusion.1
  356.8 77.0 %all-reduce.1 = (f32[8]{0:T(128)S(1)}, f32[8]{0:T(128)S(1)}) all-reduce(f32[8]{0:T(128)S(1)} %get-tuple-element.8, f32[8]{0:T(128)S(1)} %get-tuple-element.7), channel_id=1, replica_groups=mesh['row'=16,'col'=16] {'row','col'}, use_global_device_ids=true, to_apply=%region_8.11 | all-reduce | flops 16 | bytes 128 | tf_op jit(solution)/shard_map/psum | solution.py:55
  434.1 61.9 %all-gather.2 = f32[256,32,8]{1,2,0:T(8,128)S(1)} all-gather(f32[1,32,8]{1,2,0:T(8,128)S(1)} %convolution_bitcast_fusion.19), channel_id=1, replica_groups=mesh['row'=16,'col'=16] {'row','col'}, dimensions={0}, use_global_device_ids=true | all-gather | bytes 263168 | tf_op jit(solution)/shard_map/all_gather | solution.py:100
  498.0 73.7 %psum.61 = f32[8]{0:T(128)S(1)} all-reduce(f32[8]{0:T(128)S(1)} %get-tuple-element.33), channel_id=1, replica_groups=mesh['row'=16,'col'=16] {'row','col'}, use_global_device_ids=true, to_apply=%region_13.16 | all-reduce | flops 8 | bytes 64 | tf_op jit(solution)/shard_map/psum | solution.py:118
  573.4 3.8 collective-permute-start.10
  583.8 3.8 convolution_bitcast_fusion.13
  588.4 4.0 convolution_bitcast_fusion.12
  596.4 3.6 convolution_bitcast_fusion
  601.1 3.9 scatter_custom_fusion.2
  605.5 77.2 %all-reduce = (f32[8]{0:T(128)S(1)}, f32[8]{0:T(128)S(1)}) all-reduce(f32[8]{0:T(128)S(1)} %get-tuple-element.6, f32[8]{0:T(128)S(1)} %get-tuple-element.5), channel_id=1, replica_groups=mesh['row'=16,'col'=16] {'row','col'}, use_global_device_ids=true, to_apply=%region_15.18 | all-reduce | flops 16 | bytes 128 | tf_op jit(solution)/shard_map/psum | solution.py:55
  683.7 61.3 %all-gather.3 = f32[256,32,8]{1,2,0:T(8,128)S(1)} all-gather(f32[1,32,8]{1,2,0:T(8,128)S(1)} %convolution_bitcast_fusion.18), channel_id=1, replica_groups=mesh['row'=16,'col'=16] {'row','col'}, dimensions={0}, use_global_device_ids=true | all-gather | bytes 263168 | tf_op jit(solution)/shard_map/all_gather | solution.py:100
  (161 shorter events, 55.3 us)
Async XLA Ops:
  0.6 71.3 %copy-start = (f32[32,8192]{1,0:T(8,128)S(1)}, f32[32,8192]{1,0:T(8,128)}, u32[]{:S(2)}) copy-start(f32[32,8192]{1,0:T(8,128)} %param.19) | copy-start | bytes 3145732
  0.6 72.2 %copy-start.8 = (f32[8,2048]{1,0:T(8,128)S(1)}, f32[8,2048]{1,0:T(8,128)}, u32[]{:S(2)}) copy-start(f32[8,2048]{1,0:T(8,128)} %param.13) | copy-start | bytes 196612
  0.7 72.2 %copy-start.7 = (f32[32,2048]{1,0:T(8,128)S(1)}, f32[32,2048]{1,0:T(8,128)}, u32[]{:S(2)}) copy-start(f32[32,2048]{1,0:T(8,128)} %param.18) | copy-start | bytes 786436
  3.4 80.1 %copy-start.11 = (s32[16,4]{0,1:T(4,128)S(1)}, s32[16,4]{0,1:T(4,128)}, u32[]{:S(2)}) copy-start(s32[16,4]{0,1:T(4,128)} %param.15) | copy-start | bytes 772
  3.4 80.3 %copy-start.10 = (s32[16,4]{0,1:T(4,128)S(1)}, s32[16,4]{0,1:T(4,128)}, u32[]{:S(2)}) copy-start(s32[16,4]{0,1:T(4,128)} %param.17) | copy-start | bytes 772
  3.4 80.5 %copy-start.13 = (s32[1,4]{1,0:T(1,128)S(1)}, s32[1,4]{1,0:T(1,128)}, u32[]{:S(2)}) copy-start(s32[1,4]{1,0:T(1,128)} %param.21) | copy-start | bytes 52
  74.7 27.1 %collective-permute-start = (f32[8,1,128]{2,0,1:T(8,128)S(1)}, f32[8,1,128]{2,0,1:T(8,128)S(1)}, u32[]{:S(2)}, u32[]{:S(2)}) collective-permute-start(f32[8,1,128]{2,0,1:T(8,128)S(1)} %copy.118), channel_id=1, source_target_pairs={{0,16},{16,32},{32,48},{48,64},{64,80},{80,96},{96,112},{112,128},... | collective-permute-start | bytes 12296 | tf_op jit(solution)/shard_map/ppermute | solution.py:20
  77.4 24.4 %collective-permute-start.1 = (f32[8,1,128]{2,0,1:T(8,128)S(1)}, f32[8,1,128]{2,0,1:T(8,128)S(1)}, u32[]{:S(2)}, u32[]{:S(2)}) collective-permute-start(f32[8,1,128]{2,0,1:T(8,128)S(1)} %copy.119), channel_id=1, source_target_pairs={{16,0},{32,16},{48,32},{64,48},{80,64},{96,80},{112,96},{128,112},... | collective-permute-start | bytes 12296 | tf_op jit(solution)/shard_map/ppermute | solution.py:22
  78.8 23.0 %collective-permute-start.2 = (f32[8,1,128]{2,0,1:T(8,128)S(1)}, f32[8,1,128]{2,0,1:T(8,128)S(1)}, u32[]{:S(2)}, u32[]{:S(2)}) collective-permute-start(f32[8,1,128]{2,0,1:T(8,128)S(1)} %copy.120), channel_id=1, source_target_pairs={{0,1},{1,2},{2,3},{3,4},{4,5},{5,6},{6,7},{7,8},{8,9},{9,10},{10,1... | collective-permute-start | bytes 12296 | tf_op jit(solution)/shard_map/ppermute | solution.py:20
  80.8 21.1 %collective-permute-start.3 = (f32[8,1,128]{2,0,1:T(8,128)S(1)}, f32[8,1,128]{2,0,1:T(8,128)S(1)}, u32[]{:S(2)}, u32[]{:S(2)}) collective-permute-start(f32[8,1,128]{2,0,1:T(8,128)S(1)} %copy.121), channel_id=1, source_target_pairs={{1,0},{2,1},{3,2},{4,3},{5,4},{6,5},{7,6},{8,7},{9,8},{10,9},{11,1... | collective-permute-start | bytes 12296 | tf_op jit(solution)/shard_map/ppermute | solution.py:22
  89.3 4.2 copy-start.1
  89.4 8.0 %copy-start.4 = (f32[8192,128]{1,0:T(8,128)S(1)}, f32[8192,128]{1,0:T(8,128)}, u32[]{:S(2)}) copy-start(f32[8192,128]{1,0:T(8,128)} %param.14) | copy-start | bytes 12582916
  93.4 8.0 %copy-start.12 = (s32[4,128]{1,0:T(4,128)S(1)}, s32[4,128]{1,0:T(4,128)}, u32[]{:S(2)}) copy-start(s32[4,128]{1,0:T(4,128)} %param.20) | copy-start | bytes 6148
  324.5 27.4 %collective-permute-start.4 = (f32[8,1,128]{2,0,1:T(8,128)S(1)}, f32[8,1,128]{2,0,1:T(8,128)S(1)}, u32[]{:S(2)}, u32[]{:S(2)}) collective-permute-start(f32[8,1,128]{2,0,1:T(8,128)S(1)} %copy.122), channel_id=1, source_target_pairs={{0,16},{16,32},{32,48},{48,64},{64,80},{80,96},{96,112},{112,128},... | collective-permute-start | bytes 12296 | tf_op jit(solution)/shard_map/ppermute | solution.py:20
  326.2 25.8 %collective-permute-start.5 = (f32[8,1,128]{2,0,1:T(8,128)S(1)}, f32[8,1,128]{2,0,1:T(8,128)S(1)}, u32[]{:S(2)}, u32[]{:S(2)}) collective-permute-start(f32[8,1,128]{2,0,1:T(8,128)S(1)} %copy.123), channel_id=1, source_target_pairs={{16,0},{32,16},{48,32},{64,48},{80,64},{96,80},{112,96},{128,112},... | collective-permute-start | bytes 12296 | tf_op jit(solution)/shard_map/ppermute | solution.py:22
  327.5 24.5 %collective-permute-start.6 = (f32[8,1,128]{2,0,1:T(8,128)S(1)}, f32[8,1,128]{2,0,1:T(8,128)S(1)}, u32[]{:S(2)}, u32[]{:S(2)}) collective-permute-start(f32[8,1,128]{2,0,1:T(8,128)S(1)} %copy.124), channel_id=1, source_target_pairs={{0,1},{1,2},{2,3},{3,4},{4,5},{5,6},{6,7},{7,8},{8,9},{9,10},{10,1... | collective-permute-start | bytes 12296 | tf_op jit(solution)/shard_map/ppermute | solution.py:20
  332.1 19.9 %collective-permute-start.7 = (f32[8,1,128]{2,0,1:T(8,128)S(1)}, f32[8,1,128]{2,0,1:T(8,128)S(1)}, u32[]{:S(2)}, u32[]{:S(2)}) collective-permute-start(f32[8,1,128]{2,0,1:T(8,128)S(1)} %copy.125), channel_id=1, source_target_pairs={{1,0},{2,1},{3,2},{4,3},{5,4},{6,5},{7,6},{8,7},{9,8},{10,9},{11,1... | collective-permute-start | bytes 12296 | tf_op jit(solution)/shard_map/ppermute | solution.py:22
  339.6 8.0 %copy-start.5 = (f32[8192,128]{1,0:T(8,128)S(1)}, f32[8192,128]{1,0:T(8,128)}, u32[]{:S(2)}) copy-start(f32[8192,128]{1,0:T(8,128)} %param.14) | copy-start | bytes 12582916
  573.4 27.4 %collective-permute-start.10 = (f32[8,1,128]{2,0,1:T(8,128)S(1)}, f32[8,1,128]{2,0,1:T(8,128)S(1)}, u32[]{:S(2)}, u32[]{:S(2)}) collective-permute-start(f32[8,1,128]{2,0,1:T(8,128)S(1)} %copy.128), channel_id=1, source_target_pairs={{0,1},{1,2},{2,3},{3,4},{4,5},{5,6},{6,7},{7,8},{8,9},{9,10},{10,1... | collective-permute-start | bytes 12296 | tf_op jit(solution)/shard_map/ppermute | solution.py:20
  577.3 23.5 %collective-permute-start.11 = (f32[8,1,128]{2,0,1:T(8,128)S(1)}, f32[8,1,128]{2,0,1:T(8,128)S(1)}, u32[]{:S(2)}, u32[]{:S(2)}) collective-permute-start(f32[8,1,128]{2,0,1:T(8,128)S(1)} %copy.129), channel_id=1, source_target_pairs={{1,0},{2,1},{3,2},{4,3},{5,4},{6,5},{7,6},{8,7},{9,8},{10,9},{11,1... | collective-permute-start | bytes 12296 | tf_op jit(solution)/shard_map/ppermute | solution.py:22
  579.3 21.5 %collective-permute-start.8 = (f32[8,1,128]{2,0,1:T(8,128)S(1)}, f32[8,1,128]{2,0,1:T(8,128)S(1)}, u32[]{:S(2)}, u32[]{:S(2)}) collective-permute-start(f32[8,1,128]{2,0,1:T(8,128)S(1)} %copy.126), channel_id=1, source_target_pairs={{0,16},{16,32},{32,48},{48,64},{64,80},{80,96},{96,112},{112,128},... | collective-permute-start | bytes 12296 | tf_op jit(solution)/shard_map/ppermute | solution.py:20
  581.3 19.5 %collective-permute-start.9 = (f32[8,1,128]{2,0,1:T(8,128)S(1)}, f32[8,1,128]{2,0,1:T(8,128)S(1)}, u32[]{:S(2)}, u32[]{:S(2)}) collective-permute-start(f32[8,1,128]{2,0,1:T(8,128)S(1)} %copy.127), channel_id=1, source_target_pairs={{16,0},{32,16},{48,32},{64,48},{80,64},{96,80},{112,96},{128,112},... | collective-permute-start | bytes 12296 | tf_op jit(solution)/shard_map/ppermute | solution.py:22
  588.4 8.0 %copy-start.6 = (f32[8192,128]{1,0:T(8,128)S(1)}, f32[8192,128]{1,0:T(8,128)}, u32[]{:S(2)}) copy-start(f32[8192,128]{1,0:T(8,128)} %param.14) | copy-start | bytes 12582916
  683.5 64.1 %copy-start.9 = (f32[8,2048]{1,0:T(8,128)}, f32[8,2048]{1,0:T(8,128)S(1)}, u32[]{:S(2)}) copy-start(f32[8,2048]{1,0:T(8,128)S(1)} %get-tuple-element.29) | copy-start | bytes 196612
  (2 other events, 8.3 us)
where the time goes:
time: 753 us; the launch traced here: 748 us
  blocking collectives  633 us (84%)
  matrix products  54.8 us (7%)
  starting transfers between devices  27.5 us (4%)
  other arithmetic  17 us (2%)
  local copies, waits for them, and re-layouts  14.1 us (2%)
    all_gather x4, blocking collectives, precondition(): lax.all_gather(coefficients, ('row', 'col'), axis=1, tiled=True)  252 us
    psum x3, blocking collectives, pair_totals(): lax.psum((jnp.sum(first_field * second_field, axis=1), jnp.sum(third_fiel...  232 us
    psum x2, blocking collectives, shards(): cross_sum = lax.psum(jnp.sum(correction * image, axis=1), ('row', 'col'))  149 us
    dot_general x6, matrix products, sparse_forward(): product = jnp.einsum('lbkw,bkwv->lbv', picked, tile_set, precision=PRECISE)  23.5 us
    dot_general x6, matrix products, sparse_backward(): product = jnp.einsum('lbv,bkwv->lbkw', pieces, tile_set, precision=PRECISE)  21.4 us
    ppermute x6, starting transfers between devices, with_halo(): lax.ppermute(tail, axis, [(i, (i + 1) % count) for i in range(ends)])  16.4 us
  transfers between devices with their start and end apart: 12, of which 0 were waited for; matrix products, arithmetic and copies ran while one was open for 7% of the time, Pallas kernels for 0%

commit v1 on v0

v1 whole, which is shorter than its diff:
```python
import functools

import jax
import jax.numpy as jnp
from jax import lax
from jax.experimental import pallas as pl
from jax.experimental.pallas import tpu as pltpu
from jax.sharding import PartitionSpec as P

ITERS = 3
GRID = 16
LOADS = 8
NB = 16
TPR = 4
TILE = 128
M = 2048
DEFL = 32
FACE = 128
SLOTS = 4 * FACE
KROW = GRID * DEFL
MESH = pl.DeviceIdType.MESH
F32 = jnp.float32
BF16 = jnp.bfloat16


def dot_nn(a, b):
    return lax.dot_general(a, b, (((1,), (0,)), ((), ())), preferred_element_type=F32)


def dot_nt(a, b):
    return lax.dot_general(a, b, (((1,), (1,)), ((), ())), preferred_element_type=F32)


def parts(value):
    high = value.astype(BF16).astype(F32)
    return jnp.concatenate([high, value - high], axis=0).astype(BF16)


def fold(value):
    half = value.shape[0] // 2
    return value[:half] + value[half:]


def lane_ids(shape):
    return lax.broadcasted_iota(jnp.int32, shape, 1)


def row_ids(shape):
    return lax.broadcasted_iota(jnp.int32, shape, 0)


def kernel(
    rhs, flex, flex_cols, stiff, stiff_cols, defl, coarse, face_rows, face_len,
    x_ref, r_ref, z_ref,
    flex_f, stiff_f, defl_f, coarse_f, faces,
    flex_t, stiff_t, flex_s, stiff_s, defl_t, trace_t, coarse_h, coarse_l, pick,
    blocks_a, blocks_b, spread,
    p_ref, q_ref, w_ref, tr_r, tr_z, tr_p, tr_q, e_r, e_q, s1_ref,
    recv1, send2, recv2, halo_out, halo_in,
    load_sem, wsend, wrecv, send1_sem, recv1_sem, send2_sem, recv2_sem, hsend_sem, hrecv_sem,
):
    i = lax.axis_index("row")
    j = lax.axis_index("col")

    loads = [
        pltpu.make_async_copy(rhs, r_ref, load_sem.at[0]),
        pltpu.make_async_copy(defl, defl_f, load_sem.at[1]),
        pltpu.make_async_copy(face_rows, faces, load_sem.at[2]),
        pltpu.make_async_copy(flex, flex_f, load_sem.at[3]),
        pltpu.make_async_copy(stiff, stiff_f, load_sem.at[4]),
        pltpu.make_async_copy(
            coarse.at[:, pl.ds(pl.multiple_of(i * KROW, KROW), KROW)], coarse_f.at[i], load_sem.at[5]
        ),
    ]
    for load in loads:
        load.start()

    barrier = pltpu.get_barrier_semaphore()

    def greet(step, carry):
        pl.semaphore_signal(barrier, inc=1, device_id=((i + step) % GRID, j), device_id_type=MESH)
        pl.semaphore_signal(barrier, inc=1, device_id=(i, (j + step) % GRID), device_id_type=MESH)
        return carry

    lax.fori_loop(1, GRID, greet, 0)
    pl.semaphore_wait(barrier, 2 * (GRID - 1))

    def coarse_copy(there, slot):
        return pltpu.make_async_remote_copy(
            src_ref=coarse.at[:, pl.ds(pl.multiple_of(there * KROW, KROW), KROW)],
            dst_ref=coarse_f.at[slot],
            send_sem=wsend.at[there],
            recv_sem=wrecv.at[slot],
            device_id=(there, j),
            device_id_type=MESH,
        )

    def send_coarse(step, carry):
        coarse_copy((i + step) % GRID, i).start()
        return carry

    lax.fori_loop(1, GRID, send_coarse, 0)

    lane8 = lane_ids((LOADS, 128))

    def copy1(phase, there, slot):
        return pltpu.make_async_remote_copy(
            src_ref=recv1.at[phase, j],
            dst_ref=recv1.at[phase, slot],
            send_sem=send1_sem.at[there],
            recv_sem=recv1_sem.at[phase, slot],
            device_id=(i, there),
            device_id_type=MESH,
        )

    def copy2(phase, there, slot):
        return pltpu.make_async_remote_copy(
            src_ref=send2.at[there],
            dst_ref=recv2.at[phase, slot],
            send_sem=send2_sem.at[there],
            recv_sem=recv2_sem.at[phase, slot],
            device_id=(there, j),
            device_id_type=MESH,
        )

    def gather_start(phase, coefficients, sums):
        payload = jnp.where(lane8 < DEFL, coefficients, 0.0)
        for place, value in enumerate(sums):
            payload = jnp.where(lane8 == DEFL + place, value, payload)
        recv1[phase, j] = payload

        def go(step, carry):
            copy1(phase, (j + step) % GRID, j).start()
            return carry

        lax.fori_loop(1, GRID, go, 0)

    def gather_finish(phase, before_matmul=None):
        def take(step, carry):
            other = (j + step) % GRID
            copy1(phase, other, other).wait_recv()
            return carry

        lax.fori_loop(1, GRID, take, 0)
        total = jnp.zeros((LOADS, 128), F32)
        groups = []
        for group in range(4):
            gathered = None
            for place in range(4):
                payload = recv1[phase, group * 4 + place]
                total = total + payload
                moved = jnp.where(lane8 < DEFL, payload, 0.0)
                if place:
                    moved = pltpu.roll(moved, place * DEFL, 1)
                gathered = moved if gathered is None else gathered + moved
            groups.append(gathered)
        if before_matmul is not None:
            before_matmul()
        operand = parts(jnp.concatenate(groups, axis=1))
        partial = fold(dot_nt(operand, coarse_h[...]) + dot_nt(operand, coarse_l[...]))
        total = jnp.where((lane8 >= DEFL) & (lane8 < 2 * DEFL), total, 0.0)
        rolled = [total] + [pltpu.roll(total, place * DEFL, 1) for place in range(1, 4)]
        for target in range(GRID):
            tile = partial[:, (target // 4) * 128 : (target // 4 + 1) * 128]
            send2[target] = jnp.where(lane8 // DEFL == target % 4, tile, rolled[target % 4])

        def go(step, carry):
            copy2(phase, (i + step) % GRID, i).start()
            return carry

        lax.fori_loop(1, GRID, go, 0)
        recv2[phase, i] = send2[i]

        def settle(step, carry):
            other = (j + step) % GRID
            copy1(phase, other, other).wait_send()
            return carry

        lax.fori_loop(1, GRID, settle, 0)

        def take2(step, carry):
            other = (i + step) % GRID
            copy2(phase, other, other).wait_recv()
            return carry

        lax.fori_loop(1, GRID, take2, 0)
        result = recv2[phase, 0]
        for source in range(1, GRID):
            result = result + recv2[phase, source]
        turned = result
        for place in range(1, 4):
            turned = jnp.where(i % 4 == place, pltpu.roll(result, 128 - place * DEFL, 1), turned)

        def settle2(step, carry):
            other = (i + step) % GRID
            copy2(phase, other, other).wait_send()
            return carry

        lax.fori_loop(1, GRID, settle2, 0)
        return turned

    def coefficients_of(product):
        summed = fold(product)
        return summed + pltpu.roll(summed, 128 - DEFL, 1)

    loads[0].wait()
    loads[1].wait()
    defl_high = defl_f[...].astype(BF16)
    defl_low = (defl_f[...] - defl_high.astype(F32)).astype(BF16)
    defl_t[0:DEFL] = defl_high
    defl_t[DEFL : 2 * DEFL] = defl_low
    defl_t[2 * DEFL :] = jnp.zeros((128 - 2 * DEFL, M), BF16)
    start_parts = parts(r_ref[...])
    gather_start(0, coefficients_of(dot_nt(start_parts, defl_t[...])), ())

    loads[2].wait()

    def build_pick(block, carry):
        start = pl.multiple_of(block * TILE, TILE)
        rows = row_ids((TILE, FACE)) + start
        for face in range(4):
            hit = rows == faces[face : face + 1, :]
            pick[pl.ds(start, TILE), face * FACE : (face + 1) * FACE] = jnp.where(hit, 1.0, 0.0).astype(BF16)
        return carry

    lax.fori_loop(0, NB, build_pick, 0)
    both = dot_nn(jnp.concatenate([start_parts, defl_t[0 : 2 * DEFL]], axis=0), pick[...])
    tr_r[...] = both[0:LOADS] + both[LOADS : 2 * LOADS]
    trace_t[0 : 2 * DEFL] = parts(both[2 * LOADS : 2 * LOADS + DEFL] + both[2 * LOADS + DEFL :])
    trace_t[2 * DEFL :] = jnp.zeros((128 - 2 * DEFL, SLOTS), BF16)

    def build_spread(columns, target):
        lanes = lane_ids((LOADS, 128))
        rows = row_ids((NB * LOADS, 128))
        wide = lane_ids((NB * LOADS, 128))
        for tile in range(4):
            named = jnp.zeros((LOADS, 128), jnp.int32)
            for place in range(16):
                index = tile * 16 + place
                named = jnp.where(lanes // LOADS == place, columns[index // TPR, index % TPR], named)
            hit = (rows // LOADS == named[0:1, :]) & (rows % LOADS == wide % LOADS)
            target[:, tile * 128 : (tile + 1) * 128] = jnp.where(hit, 1.0, 0.0).astype(BF16)

    build_spread(flex_cols, flex_s)
    build_spread(stiff_cols, stiff_s)

    def convert(source, target):
        def one(block, carry):
            tiles = source[pl.ds(pl.multiple_of(block * TPR * TILE, TPR * TILE), TPR * TILE), :]
            high = tiles.astype(BF16)
            target[block, :, 0:TILE] = high
            target[block, :, TILE : 2 * TILE] = (tiles - high.astype(F32)).astype(BF16)
            return carry

        lax.fori_loop(0, NB, one, 0)

    loads[3].wait()
    convert(flex_f, flex_t)
    loads[4].wait()
    convert(stiff_f, stiff_t)

    def coarse_ready():
        loads[5].wait()

        def take(step, carry):
            other = (i + step) % GRID
            coarse_copy(other, other).wait_recv()
            return carry

        lax.fori_loop(1, GRID, take, 0)

        def one(block, carry):
            rows = coarse_f[block]
            high = rows.astype(BF16)
            start = pl.multiple_of(block * DEFL, DEFL)
            coarse_h[pl.ds(start, DEFL), :] = high
            coarse_l[pl.ds(start, DEFL), :] = (rows - high.astype(F32)).astype(BF16)
            return carry

        lax.fori_loop(0, GRID, one, 0)

    zeros = jnp.zeros((LOADS, M), F32)
    p_ref[...] = zeros
    q_ref[...] = zeros
    x_ref[...] = zeros
    tr_p[...] = jnp.zeros((LOADS, SLOTS), F32)
    tr_q[...] = jnp.zeros((LOADS, SLOTS), F32)
    e_q[...] = jnp.zeros((LOADS, 128), F32)
    s1_ref[...] = jnp.ones((LOADS, 128), F32)

    first = gather_finish(0, coarse_ready)
    e_r[...] = jnp.where(lane8 < DEFL, first, 0.0)

    def settle_coarse(step, carry):
        other = (i + step) % GRID
        coarse_copy(other, other).wait_send()
        return carry

    lax.fori_loop(1, GRID, settle_coarse, 0)

    def energy_parts():
        energy = e_r[...]
        return parts(energy + pltpu.roll(energy, DEFL, 1))[:, 0 : 2 * DEFL]

    def face_copy(step, face, device, slot):
        return pltpu.make_async_remote_copy(
            src_ref=halo_out.at[face],
            dst_ref=halo_in.at[step, slot],
            send_sem=hsend_sem.at[face],
            recv_sem=hrecv_sem.at[step, slot],
            device_id=device,
            device_id_type=MESH,
        )

    sides = (
        (i > 0, (i - 1, j), 1),
        (i < GRID - 1, (i + 1, j), 0),
        (j > 0, (i, j - 1), 3),
        (j < GRID - 1, (i, j + 1), 2),
    )

    def store_blocks(target, block, value):
        target[block] = parts(value)

    def forward(source, tiles, columns, target):
        for block in range(NB):
            operand = jnp.concatenate([source[columns[block, k]] for k in range(TPR)], axis=1)
            product = fold(dot_nn(operand, tiles[block]))
            store_blocks(target, block, product[:, 0:TILE] + product[:, TILE : 2 * TILE])

    def backward(source, tiles, selector):
        for block in range(NB):
            piece = source[block]
            product = fold(dot_nt(jnp.concatenate([piece, piece], axis=1), tiles[block]))
            stacked = jnp.concatenate(
                [product[:, k * TILE : (k + 1) * TILE] for k in range(TPR)], axis=0
            )
            high = stacked.astype(BF16)
            rows = slice(block * TPR * LOADS, (block + 1) * TPR * LOADS)
            spread[rows, 0:TILE] = high
            spread[rows, TILE : 2 * TILE] = (stacked - high.astype(F32)).astype(BF16)
        summed = dot_nn(selector[...], spread[...])
        return summed[:, 0:TILE] + summed[:, TILE : 2 * TILE]

    def correct(energy):
        z_ref[...] = r_ref[...] + fold(dot_nn(energy, defl_t[0 : 2 * DEFL]))

    live = jnp.concatenate(
        [jnp.where(lane8 < face_len[0, face], 1.0, 0.0) for face in range(4)], axis=1
    )

    def iterate(step, carry):
        energy = energy_parts()
        traces = tr_r[...] + fold(dot_nn(energy, trace_t[0 : 2 * DEFL]))
        tr_z[...] = traces
        for face in range(4):
            halo_out[face] = traces[:, face * FACE : (face + 1) * FACE]
        for face, (inside, device, slot) in enumerate(sides):

            @pl.when(inside)
            def _():
                face_copy(step, face, device, slot).start()

        correct(energy)
        z = z_ref[...]
        for block in range(NB):
            store_blocks(blocks_a, block, z[:, block * TILE : (block + 1) * TILE])
        forward(blocks_a, flex_t, flex_cols, blocks_b)
        forward(blocks_b, stiff_t, stiff_cols, blocks_a)
        middle = backward(blocks_a, stiff_t, stiff_s)
        for block in range(NB):
            store_blocks(blocks_b, block, middle[block * LOADS : (block + 1) * LOADS])
        local = backward(blocks_b, flex_t, flex_s)
        local = jnp.concatenate(
            [local[block * LOADS : (block + 1) * LOADS] for block in range(NB)], axis=1
        )
        u = z_ref[...] + local
        w_ref[...] = u
        z = z_ref[...]
        p = p_ref[...]
        r = r_ref[...]
        sum_zu = jnp.sum(z * u, axis=1, keepdims=True)
        sum_pu = jnp.sum(p * u, axis=1, keepdims=True)
        sum_rz = jnp.sum(r * z, axis=1, keepdims=True)
        sum_rp = jnp.sum(r * p, axis=1, keepdims=True)
        sum_zq = jnp.sum(z * q_ref[...], axis=1, keepdims=True)
        product = dot_nt(parts(u), defl_t[...])

        for face, (inside, device, slot) in enumerate(sides):

            @pl.when(inside)
            def _():
                face_copy(step, slot, device, face).wait_recv()

        partner = jnp.concatenate([halo_in[step, face] for face in range(4)], axis=1)
        jump = jnp.where(live > 0.5, tr_z[...] - partner, 0.0)
        jump_parts = parts(jump)
        product = product + dot_nt(jump_parts, trace_t[...])
        sum_zw = sum_zu + jnp.sum(tr_z[...] * jump, axis=1, keepdims=True)
        sum_pw = sum_pu + jnp.sum(tr_p[...] * jump, axis=1, keepdims=True)
        gather_start(step + 1, coefficients_of(product), (sum_zw, sum_pw, sum_rz, sum_rp, sum_zq))

        w = w_ref[...] + fold(dot_nt(jump_parts, pick[...]))
        w_ref[...] = w
        traced = fold(dot_nn(parts(w), pick[...]))
        for face, (inside, device, slot) in enumerate(sides):

            @pl.when(inside)
            def _():
                face_copy(step, face, device, slot).wait_send()

        gathered = gather_finish(step + 1)

        def total(place):
            return gathered[:, DEFL + place : DEFL + place + 1]

        beta = -total(4) / s1_ref[:, 0:1]
        curvature = total(0) + beta * total(1)
        alpha = (total(2) + beta * total(3)) / curvature
        s1_ref[...] = jnp.broadcast_to(curvature, (LOADS, 128))
        energy_q = jnp.where(lane8 < DEFL, gathered, 0.0) + beta * e_q[...]
        e_q[...] = energy_q
        e_r[...] = e_r[...] - alpha * energy_q
        trace_q = traced + beta * tr_q[...]
        tr_q[...] = trace_q
        tr_p[...] = tr_z[...] + beta * tr_p[...]
        tr_r[...] = tr_r[...] - alpha * trace_q
        direction = z_ref[...] + beta * p_ref[...]
        image = w_ref[...] + beta * q_ref[...]
        p_ref[...] = direction
        q_ref[...] = image
        x_ref[...] = x_ref[...] + alpha * direction
        r_ref[...] = r_ref[...] - alpha * image
        return carry

    lax.fori_loop(0, ITERS, iterate, 0)
    correct(energy_parts())


def shards(*args):
    anywhere = pl.BlockSpec(memory_space=pl.ANY)
    scalars = pl.BlockSpec(memory_space=pltpu.SMEM)
    vector = pl.BlockSpec(memory_space=pltpu.VMEM)
    field = jax.ShapeDtypeStruct((LOADS, M), F32)
    vmem = pltpu.VMEM
    dma = pltpu.SemaphoreType.DMA
    return pl.pallas_call(
        kernel,
        out_shape=(field, field, field),
        in_specs=[
            anywhere, anywhere, scalars, anywhere, scalars, anywhere, anywhere, anywhere, scalars,
        ],
        out_specs=(vector, vector, vector),
        scratch_shapes=[
            vmem((NB * TPR * TILE, TILE), F32),
            vmem((NB * TPR * TILE, TILE), F32),
            vmem((DEFL, M), F32),
            vmem((GRID, DEFL, KROW), F32),
            vmem((4, FACE), jnp.int32),
            vmem((NB, TPR * TILE, 2 * TILE), BF16),
            vmem((NB, TPR * TILE, 2 * TILE), BF16),
            vmem((NB * LOADS, NB * TPR * LOADS), BF16),
            vmem((NB * LOADS, NB * TPR * LOADS), BF16),
            vmem((128, M), BF16),
            vmem((128, SLOTS), BF16),
            vmem((KROW, KROW), BF16),
            vmem((KROW, KROW), BF16),
            vmem((M, SLOTS), BF16),
            vmem((NB, 2 * LOADS, TILE), BF16),
            vmem((NB, 2 * LOADS, TILE), BF16),
            vmem((NB * TPR * LOADS, 2 * TILE), BF16),
            vmem((LOADS, M), F32),
            vmem((LOADS, M), F32),
            vmem((LOADS, M), F32),
            vmem((LOADS, SLOTS), F32),
            vmem((LOADS, SLOTS), F32),
            vmem((LOADS, SLOTS), F32),
            vmem((LOADS, SLOTS), F32),
            vmem((LOADS, 128), F32),
            vmem((LOADS, 128), F32),
            vmem((LOADS, 128), F32),
            vmem((ITERS + 1, GRID, LOADS, 128), F32),
            vmem((GRID, LOADS, 128), F32),
            vmem((ITERS + 1, GRID, LOADS, 128), F32),
            vmem((4, LOADS, FACE), F32),
            vmem((ITERS, 4, LOADS, FACE), F32),
            dma((6,)),
            dma((GRID,)),
            dma((GRID,)),
            dma((GRID,)),
            dma((ITERS + 1, GRID)),
            dma((GRID,)),
            dma((ITERS + 1, GRID)),
            dma((4,)),
            dma((ITERS, 4)),
        ],
        compiler_params=pltpu.CompilerParams(
            collective_id=0, has_side_effects=True, vmem_limit_bytes=56 * 1024 * 1024
        ),
        name="feti",
    )(*args)


def solution(mesh):
    return jax.shard_map(
        shards,
        mesh=mesh,
        in_specs=(
            P("row", "col"),
            P("row", "col"),
            P("row", "col"),
            P("row", "col"),
            P("row", "col"),
            P("row", "col"),
            P(("row", "col"), None),
            P("row", "col"),
            P("row", "col"),
        ),
        out_specs=(P("row", "col"), P("row", "col"), P("row", "col")),
        check_vma=False,
    )
```

time: 753 us -> 89.3 us (0.12)
  blocking collectives: 633 us -> 0 us
  Pallas kernels: 0 us -> 81.2 us
  matrix products: 54.8 us -> 0 us
  starting transfers between devices: 27.5 us -> 0 us
  other arithmetic: 17 us -> 0 us
    psum x5 -> x0, blocking collectives: 381 us -> none  [the longest x3 232 us: pair_totals(): lax.psum((jnp.sum(first_field * second_field, axis=1), jnp.sum(third_fiel...]
    all_gather x4 -> x0, blocking collectives: 252 us -> none  [precondition(): lax.all_gather(coefficients, ('row', 'col'), axis=1, tiled=True)]
    pallas_call x0 -> x1, Pallas kernels: none -> 81.2 us  [shards(): pl.pallas_call(kernel, out_shape=(field, field, field), in_specs=[anywher...]
    dot_general x30 -> x0, matrix products: 54.8 us -> none  [the longest x6 23.5 us: sparse_forward(): product = jnp.einsum('lbkw,bkwv->lbv', picked, tile_set, precision=PRECISE)]
    ppermute x12 -> x0, starting transfers between devices: 27.5 us -> none  [the longest x6 16.4 us: with_halo(): lax.ppermute(tail, axis, [(i, (i + 1) % count) for i in range(ends)])]
    scatter-add x3 -> x0, other arithmetic: 12 us -> none  [face_part(): return jnp.zeros_like(vector).at[:, flat_index].add(jump_values.reshape(l...]
  transfers between devices with their start and end apart: 12 -> 0, of which waited for: 0 -> 0; matrix products, arithmetic and copies ran while one was open for 7% -> 0% of each run, Pallas kernels for 0% -> 0%
where the time goes in v1:
time: 89.3 us; the launch traced here: 89 us
  Pallas kernels  81.2 us (91%)
  local copies, waits for them, and re-layouts  7.13 us (8%)
    pallas_call x1, Pallas kernels, shards(): pl.pallas_call(kernel, out_shape=(field, field, field), in_specs=[anywher...  81.2 us
    unnamed x5, local copies, waits for them, and re-layouts  7.13 us

profile of v1, /device:TPU:1, one launch (start us, length us, event | category | flops | bytes accessed | tf_op | source)
XLA Modules:
  0.0 89.0 jit_solution(9481659282586046150)
XLA Ops:
  0.6 1.4 %copy.12.flex_cols = s32[16,4]{1,0:T(8,128)} copy(s32[16,4]{0,1:T(4,128)} %param.11) | data formatting | bytes 512 | tf_op args[2]
  2.0 1.4 %copy.13.stiff_cols = s32[16,4]{1,0:T(8,128)} copy(s32[16,4]{0,1:T(4,128)} %param.13) | data formatting | bytes 512 | tf_op args[4]
  3.3 81.2 %feti.1 = (f32[8,2048]{1,0:T(8,128)}, f32[8,2048]{1,0:T(8,128)}, f32[8,2048]{1,0:T(8,128)}) custom-call(f32[8,2048]{1,0:T(8,128)} %rhs.1, f32[8192,128]{1,0:T(8,128)} %flex.1, s32[16,4]{1,0:T(8,128)} %copy.12.flex_cols, f32[8192,128]{1,0:T(8,128)} %stiff.1, s32[16,4]{1,0:T(8,128)} %copy.13.stiff_cols, f32[32,2048]{1,0:T(8,128)} %defl.1, f32[32,8192]{1,0:T(8,128)} %coarse.1, ...), custom_call_target="tpu_custom_call" | custom-call | tf_op jit(solution)/shard_map/feti/pallas_call | solution.py:447
  84.5 1.5 %copy.17 = f32[8,2048]{1,0:T(8,128)} copy(f32[8,2048]{1,0:T(8,128)} %get-tuple-element.6) | data formatting | bytes 131072
  86.0 1.5 %copy.18 = f32[8,2048]{1,0:T(8,128)} copy(f32[8,2048]{1,0:T(8,128)} %get-tuple-element.7) | data formatting | bytes 131072
  87.5 1.5 %copy.19 = f32[8,2048]{1,0:T(8,128)} copy(f32[8,2048]{1,0:T(8,128)} %get-tuple-element.8) | data formatting | bytes 131072

commit v2 on v1

v2 whole, which is shorter than its diff:
```python
import functools

import jax
import jax.numpy as jnp
from jax import lax
from jax.experimental import pallas as pl
from jax.experimental.pallas import tpu as pltpu
from jax.sharding import PartitionSpec as P

ITERS = 3
GRID = 16
LOADS = 8
NB = 16
TPR = 4
TILE = 128
M = 2048
DEFL = 32
FACE = 128
SLOTS = 4 * FACE
KROW = GRID * DEFL
MESH = pl.DeviceIdType.MESH
F32 = jnp.float32
BF16 = jnp.bfloat16


def dot_nn(a, b):
    return lax.dot_general(a, b, (((1,), (0,)), ((), ())), preferred_element_type=F32)


def dot_nt(a, b):
    return lax.dot_general(a, b, (((1,), (1,)), ((), ())), preferred_element_type=F32)


def parts(value):
    high = value.astype(BF16).astype(F32)
    return jnp.concatenate([high, value - high], axis=0).astype(BF16)


def fold(value):
    half = value.shape[0] // 2
    return value[:half] + value[half:]


def lane_ids(shape):
    return lax.broadcasted_iota(jnp.int32, shape, 1)


def row_ids(shape):
    return lax.broadcasted_iota(jnp.int32, shape, 0)


def kernel(
    rhs, flex, flex_cols, stiff, stiff_cols, defl, coarse, face_rows, face_len,
    x_ref, r_ref, z_ref,
    flex_f, stiff_f, defl_f, coarse_f, faces,
    flex_t, stiff_t, flex_s, stiff_s, defl_t, image_t, trace_t, coarse_h, coarse_l, pick,
    wide_a, wide_b, wide_spread, blocks_a, blocks_b, spread,
    a_ref, b_ref, bw_ref, p_ref, q_ref, w_ref, tr_r, tr_z, tr_w, tr_p, tr_q,
    e_r, e_q, s1_ref, alpha_ref, beta_ref,
    recv1, send2, recv2, halo_out, halo_in,
    load_sem, wsend, wrecv, send1_sem, recv1_sem, send2_sem, recv2_sem, hsend_sem, hrecv_sem,
):
    i = lax.axis_index("row")
    j = lax.axis_index("col")
    chunk = NB * TPR * TILE // 4

    def part_of(ref, index):
        return ref.at[pl.ds(index * chunk, chunk), :]

    load_r = pltpu.make_async_copy(rhs, r_ref, load_sem.at[0])
    load_z = pltpu.make_async_copy(defl, defl_f, load_sem.at[1])
    load_faces = pltpu.make_async_copy(face_rows, faces, load_sem.at[2])
    load_coarse = pltpu.make_async_copy(
        coarse.at[:, pl.ds(pl.multiple_of(i * KROW, KROW), KROW)], coarse_f.at[i], load_sem.at[3]
    )
    load_flex = [
        pltpu.make_async_copy(part_of(flex, n), part_of(flex_f, n), load_sem.at[4 + n]) for n in range(4)
    ]
    load_stiff = [
        pltpu.make_async_copy(part_of(stiff, n), part_of(stiff_f, n), load_sem.at[8 + n]) for n in range(4)
    ]
    for load in [load_r, load_z, load_faces] + load_flex + load_stiff + [load_coarse]:
        load.start()

    row_partners = []
    for dy, dx in sorted(
        [(dy, dx) for dy in range(4) for dx in range(4) if dy or dx],
        key=lambda pair: -(min(pair[0], 4 - pair[0]) + min(pair[1], 4 - pair[1])),
    ):
        row_partners.append(((i // 4 + dy) % 4) * 4 + (i % 4 + dx) % 4)
    col_partners = [
        (j + offset) % GRID for offset in sorted(range(1, GRID), key=lambda o: -min(o, GRID - o))
    ]

    barrier = pltpu.get_barrier_semaphore()
    for there in row_partners:
        pl.semaphore_signal(barrier, inc=1, device_id=(there, j), device_id_type=MESH)
    for there in col_partners:
        pl.semaphore_signal(barrier, inc=1, device_id=(i, there), device_id_type=MESH)
    pl.semaphore_wait(barrier, 2 * (GRID - 1))

    def coarse_copy(there, slot):
        return pltpu.make_async_remote_copy(
            src_ref=coarse.at[:, pl.ds(pl.multiple_of(there * KROW, KROW), KROW)],
            dst_ref=coarse_f.at[slot],
            send_sem=wsend,
            recv_sem=wrecv,
            device_id=(there, j),
            device_id_type=MESH,
        )

    for there in row_partners:
        coarse_copy(there, i).start()

    lane8 = lane_ids((LOADS, 128))

    def copy1(phase, there):
        return pltpu.make_async_remote_copy(
            src_ref=recv1.at[phase, j],
            dst_ref=recv1.at[phase, j],
            send_sem=send1_sem,
            recv_sem=recv1_sem.at[phase],
            device_id=(i, there),
            device_id_type=MESH,
        )

    def copy2(phase, there):
        return pltpu.make_async_remote_copy(
            src_ref=send2.at[there],
            dst_ref=recv2.at[phase, i],
            send_sem=send2_sem,
            recv_sem=recv2_sem.at[phase],
            device_id=(there, j),
            device_id_type=MESH,
        )

    def whole1(phase):
        slots = recv1.at[phase, pl.ds(0, GRID - 1)]
        return pltpu.make_async_remote_copy(
            src_ref=slots,
            dst_ref=slots,
            send_sem=send1_sem,
            recv_sem=recv1_sem.at[phase],
            device_id=(i, j),
            device_id_type=MESH,
        )

    def whole2(phase):
        return pltpu.make_async_remote_copy(
            src_ref=send2.at[pl.ds(0, GRID - 1)],
            dst_ref=recv2.at[phase, pl.ds(0, GRID - 1)],
            send_sem=send2_sem,
            recv_sem=recv2_sem.at[phase],
            device_id=(i, j),
            device_id_type=MESH,
        )

    def whole_coarse():
        slots = coarse_f.at[pl.ds(0, GRID - 1)]
        return pltpu.make_async_remote_copy(
            src_ref=slots,
            dst_ref=slots,
            send_sem=wsend,
            recv_sem=wrecv,
            device_id=(i, j),
            device_id_type=MESH,
        )

    def gather_start(phase, coefficients, sums):
        payload = jnp.where(lane8 < DEFL, coefficients, 0.0)
        for place, value in enumerate(sums):
            payload = jnp.where(lane8 == DEFL + place, value, payload)
        recv1[phase, j] = payload
        for there in col_partners:
            copy1(phase, there).start()

    def gather_middle(phase, before_matmul=None):
        whole1(phase).wait_recv()
        total = jnp.zeros((LOADS, 128), F32)
        groups = []
        for group in range(4):
            gathered = None
            for place in range(4):
                payload = recv1[phase, group * 4 + place]
                total = total + payload
                moved = jnp.where(lane8 < DEFL, payload, 0.0)
                if place:
                    moved = pltpu.roll(moved, place * DEFL, 1)
                gathered = moved if gathered is None else gathered + moved
            groups.append(gathered)
        if before_matmul is not None:
            before_matmul()
        operand = parts(jnp.concatenate(groups, axis=1))
        partial = fold(dot_nt(operand, coarse_h[...]) + dot_nt(operand, coarse_l[...]))
        total = jnp.where((lane8 >= DEFL) & (lane8 < 2 * DEFL), total, 0.0)
        rolled = [total] + [pltpu.roll(total, place * DEFL, 1) for place in range(1, 4)]
        for target in range(GRID):
            tile = partial[:, (target // 4) * 128 : (target // 4 + 1) * 128]
            send2[target] = jnp.where(lane8 // DEFL == target % 4, tile, rolled[target % 4])
        for there in row_partners:
            copy2(phase, there).start()
        recv2[phase, i] = send2[i]

    def gather_end(phase):
        whole2(phase).wait_recv()
        level = [recv2[phase, source] for source in range(GRID)]
        while len(level) > 1:
            level = [level[n] + level[n + 1] for n in range(0, len(level), 2)]
        result = level[0]
        turned = result
        for place in range(1, 4):
            turned = jnp.where(i % 4 == place, pltpu.roll(result, 128 - place * DEFL, 1), turned)
        whole1(phase).wait_send()
        whole2(phase).wait_send()
        return turned

    def coefficients_of(product):
        summed = fold(product)
        return summed + pltpu.roll(summed, 128 - DEFL, 1)

    load_r.wait()
    load_z.wait()
    defl_high = defl_f[...].astype(BF16)
    defl_low = (defl_f[...] - defl_high.astype(F32)).astype(BF16)
    defl_t[0:DEFL] = defl_high
    defl_t[DEFL : 2 * DEFL] = defl_low
    defl_t[2 * DEFL :] = jnp.zeros((128 - 2 * DEFL, M), BF16)
    gather_start(0, coefficients_of(dot_nt(parts(r_ref[...]), defl_t[...])), ())

    load_faces.wait()

    def build_pick(block, carry):
        start = pl.multiple_of(block * TILE, TILE)
        rows = row_ids((TILE, FACE)) + start
        for face in range(4):
            hit = rows == faces[face : face + 1, :]
            pick[pl.ds(start, TILE), face * FACE : (face + 1) * FACE] = jnp.where(hit, 1.0, 0.0).astype(BF16)
        return carry

    lax.fori_loop(0, NB, build_pick, 0)
    wide = LOADS + DEFL
    basis = parts(jnp.concatenate([r_ref[...], defl_f[...]], axis=0))
    for block in range(NB):
        wide_a[block] = basis[:, block * TILE : (block + 1) * TILE]
    both = fold(dot_nn(basis, pick[...]))
    tr_r[...] = both[0:LOADS]
    trace_t[0 : 2 * DEFL] = parts(both[LOADS:])
    trace_t[2 * DEFL :] = jnp.zeros((128 - 2 * DEFL, SLOTS), BF16)

    def build_spread(columns, target):
        lanes = lane_ids((LOADS, 128))
        rows = row_ids((NB * LOADS, 128))
        across = lane_ids((NB * LOADS, 128))
        for tile in range(4):
            named = jnp.zeros((LOADS, 128), jnp.int32)
            for place in range(16):
                index = tile * 16 + place
                named = jnp.where(lanes // LOADS == place, columns[index % TPR, index // TPR], named)
            hit = (rows // LOADS == named[0:1, :]) & (rows % LOADS == across % LOADS)
            target[:, tile * 128 : (tile + 1) * 128] = jnp.where(hit, 1.0, 0.0).astype(BF16)

    build_spread(flex_cols, flex_s)
    build_spread(stiff_cols, stiff_s)

    def convert(pending, source, target):
        for n, load in enumerate(pending):
            load.wait()

            def one(block, carry):
                tiles = source[pl.ds(pl.multiple_of(block * TPR * TILE, TPR * TILE), TPR * TILE), :]
                high = tiles.astype(BF16)
                target[block, :, 0:TILE] = high
                target[block, :, TILE : 2 * TILE] = (tiles - high.astype(F32)).astype(BF16)
                return carry

            lax.fori_loop(n * NB // 4, (n + 1) * NB // 4, one, 0)

    convert(load_flex, flex_f, flex_t)
    convert(load_stiff, stiff_f, stiff_t)

    def coarse_ready():
        load_coarse.wait()
        whole_coarse().wait_recv()

        def one(block, carry):
            rows = coarse_f[block]
            high = rows.astype(BF16)
            start = pl.multiple_of(block * DEFL, DEFL)
            coarse_h[pl.ds(start, DEFL), :] = high
            coarse_l[pl.ds(start, DEFL), :] = (rows - high.astype(F32)).astype(BF16)
            return carry

        lax.fori_loop(0, GRID, one, 0)

    def forward(source, tiles, columns, target):
        for block in range(NB):
            operand = jnp.concatenate([source[columns[k, block]] for k in range(TPR)], axis=1)
            product = fold(dot_nn(operand, tiles[block]))
            target[block] = parts(product[:, 0:TILE] + product[:, TILE : 2 * TILE])

    def backward(source, tiles, selector, space):
        groups = space.shape[0]
        for block in range(NB):
            piece = source[block]
            product = fold(dot_nt(jnp.concatenate([piece, piece], axis=1), tiles[block]))
            rows = slice(block * TPR * LOADS, (block + 1) * TPR * LOADS)
            for group in range(groups):
                loads = product[group * LOADS : (group + 1) * LOADS]
                stacked = jnp.concatenate(
                    [loads[:, k * TILE : (k + 1) * TILE] for k in range(TPR)], axis=0
                )
                high = stacked.astype(BF16)
                space[group, rows, 0:TILE] = high
                space[group, rows, TILE : 2 * TILE] = (stacked - high.astype(F32)).astype(BF16)
        summed = []
        for group in range(groups):
            product = dot_nn(selector[...], space[group])
            summed.append(product[:, 0:TILE] + product[:, TILE : 2 * TILE])
        return [
            jnp.concatenate([one[block * LOADS : (block + 1) * LOADS] for one in summed], axis=0)
            for block in range(NB)
        ]

    forward(wide_a, flex_t, flex_cols, wide_b)
    forward(wide_b, stiff_t, stiff_cols, wide_a)
    gather_middle(0, coarse_ready)
    middle = backward(wide_a, stiff_t, stiff_s, wide_spread)
    for block in range(NB):
        wide_b[block] = parts(middle[block])
    applied = backward(wide_b, flex_t, flex_s, wide_spread)
    for block in range(NB):
        cut = slice(block * TILE, (block + 1) * TILE)
        a_ref[:, cut] = r_ref[:, cut] + applied[block][0:LOADS]
        image_t[:, cut] = parts(defl_f[:, cut] + applied[block][LOADS:wide])

    zeros = jnp.zeros((LOADS, M), F32)
    for ref in (b_ref, bw_ref, p_ref, q_ref, w_ref, x_ref, z_ref):
        ref[...] = zeros
    tr_p[...] = jnp.zeros((LOADS, SLOTS), F32)
    tr_q[...] = jnp.zeros((LOADS, SLOTS), F32)
    tr_z[...] = jnp.zeros((LOADS, SLOTS), F32)
    e_q[...] = jnp.zeros((LOADS, 128), F32)
    s1_ref[...] = jnp.ones((LOADS, 128), F32)
    alpha_ref[...] = jnp.zeros((LOADS, 128), F32)
    beta_ref[...] = jnp.zeros((LOADS, 128), F32)

    e_r[...] = jnp.where(lane8 < DEFL, gather_end(0), 0.0)
    whole_coarse().wait_send()

    def energy_parts():
        energy = e_r[...]
        return parts(energy + pltpu.roll(energy, DEFL, 1))[:, 0 : 2 * DEFL]

    def face_copy(step, face, device, slot):
        return pltpu.make_async_remote_copy(
            src_ref=halo_out.at[face],
            dst_ref=halo_in.at[step, slot],
            send_sem=hsend_sem.at[face],
            recv_sem=hrecv_sem.at[step, slot],
            device_id=device,
            device_id_type=MESH,
        )

    sides = (
        (i > 0, (i - 1, j), 1),
        (i < GRID - 1, (i + 1, j), 0),
        (j > 0, (i, j - 1), 3),
        (j < GRID - 1, (i, j + 1), 2),
    )

    live = jnp.concatenate(
        [jnp.where(lane8 < face_len[0, face], 1.0, 0.0) for face in range(4)], axis=1
    )

    def advance():
        alpha = alpha_ref[:, 0:1]
        beta = beta_ref[:, 0:1]
        direction = z_ref[...] + beta * p_ref[...]
        image = w_ref[...] + beta * q_ref[...]
        p_ref[...] = direction
        q_ref[...] = image
        x_ref[...] = x_ref[...] + alpha * direction
        residual = r_ref[...] - alpha * image
        r_ref[...] = residual
        return alpha, beta, direction, image, residual

    def row_sum(value):
        return jnp.sum(value, axis=1, keepdims=True)

    def iterate(step, carry):
        energy = energy_parts()
        old_traces = tr_z[...]
        traces = tr_r[...] + fold(dot_nn(energy, trace_t[0 : 2 * DEFL]))
        tr_z[...] = traces
        for face in range(4):
            halo_out[face] = traces[:, face * FACE : (face + 1) * FACE]
        for face, (inside, device, slot) in enumerate(sides):

            @pl.when(inside)
            def _():
                face_copy(step, face, device, slot).start()

        alpha, beta, p, q, r = advance()
        tr_p[...] = old_traces + beta * tr_p[...]
        applied = bw_ref[...] + beta * b_ref[...]
        b_ref[...] = applied
        a = a_ref[...] - alpha * applied
        a_ref[...] = a
        z = r + fold(dot_nn(energy, defl_t[0 : 2 * DEFL]))
        z_ref[...] = z
        u = a + fold(dot_nn(energy, image_t[...]))
        w_ref[...] = u
        product = dot_nt(parts(u), defl_t[...])
        sum_zu = row_sum(z * u)
        sum_pu = row_sum(p * u)
        sum_rz = row_sum(r * z)
        sum_rp = row_sum(r * p)
        sum_zq = row_sum(z * q)

        for face, (inside, device, slot) in enumerate(sides):

            @pl.when(inside)
            def _():
                face_copy(step, slot, device, face).wait_recv()

        partner = jnp.concatenate([halo_in[step, face] for face in range(4)], axis=1)
        jump = jnp.where(live > 0.5, tr_z[...] - partner, 0.0)
        jump_parts = parts(jump)
        product = product + dot_nt(jump_parts, trace_t[...])
        sum_zw = sum_zu + row_sum(tr_z[...] * jump)
        sum_pw = sum_pu + row_sum(tr_p[...] * jump)
        gather_start(step + 1, coefficients_of(product), (sum_zw, sum_pw, sum_rz, sum_rp, sum_zq))

        w = w_ref[...] + fold(dot_nt(jump_parts, pick[...]))
        w_ref[...] = w
        split = parts(w)
        for block in range(NB):
            blocks_a[block] = split[:, block * TILE : (block + 1) * TILE]
        for face, (inside, device, slot) in enumerate(sides):

            @pl.when(inside)
            def _():
                face_copy(step, face, device, slot).wait_send()

        @pl.when(step < ITERS - 1)
        def _():
            tr_w[...] = fold(dot_nn(split, pick[...]))
            forward(blocks_a, flex_t, flex_cols, blocks_b)

        gather_middle(step + 1)

        @pl.when(step < ITERS - 1)
        def _():
            forward(blocks_b, stiff_t, stiff_cols, blocks_a)
            middle = backward(blocks_a, stiff_t, stiff_s, spread)
            for block in range(NB):
                blocks_b[block] = parts(middle[block])
            local = backward(blocks_b, flex_t, flex_s, spread)
            bw_ref[...] = w_ref[...] + jnp.concatenate(local, axis=1)

        gathered = gather_end(step + 1)

        def total(place):
            return gathered[:, DEFL + place : DEFL + place + 1]

        new_beta = -total(4) / s1_ref[:, 0:1]
        curvature = total(0) + new_beta * total(1)
        new_alpha = (total(2) + new_beta * total(3)) / curvature
        s1_ref[...] = jnp.broadcast_to(curvature, (LOADS, 128))
        alpha_ref[...] = jnp.broadcast_to(new_alpha, (LOADS, 128))
        beta_ref[...] = jnp.broadcast_to(new_beta, (LOADS, 128))
        energy_q = jnp.where(lane8 < DEFL, gathered, 0.0) + new_beta * e_q[...]
        e_q[...] = energy_q
        e_r[...] = e_r[...] - new_alpha * energy_q
        trace_q = tr_w[...] + new_beta * tr_q[...]
        tr_q[...] = trace_q
        tr_r[...] = tr_r[...] - new_alpha * trace_q
        return carry

    tr_w[...] = jnp.zeros((LOADS, SLOTS), F32)
    lax.fori_loop(0, ITERS, iterate, 0)
    advance()
    z_ref[...] = r_ref[...] + fold(dot_nn(energy_parts(), defl_t[0 : 2 * DEFL]))


def publish(x_in, r_in, z_in, x_out, r_out, z_out):
    x_out[...] = x_in[...]
    r_out[...] = r_in[...]
    z_out[...] = z_in[...]


def shards(rhs, flex, flex_cols, stiff, stiff_cols, defl, coarse, face_rows, face_len):
    anywhere = pl.BlockSpec(memory_space=pl.ANY)
    scalars = pl.BlockSpec(memory_space=pltpu.SMEM)
    vector = pl.BlockSpec(memory_space=pltpu.VMEM)
    field = jax.ShapeDtypeStruct((LOADS, M), F32)
    vmem = pltpu.VMEM
    dma = pltpu.SemaphoreType.DMA
    wide = 2 * (LOADS + DEFL)
    found = pl.pallas_call(
        kernel,
        out_shape=(field, field, field),
        in_specs=[
            anywhere, anywhere, scalars, anywhere, scalars, anywhere, anywhere, anywhere, scalars,
        ],
        out_specs=(vector, vector, vector),
        scratch_shapes=[
            vmem((NB * TPR * TILE, TILE), F32),
            vmem((NB * TPR * TILE, TILE), F32),
            vmem((DEFL, M), F32),
            vmem((GRID, DEFL, KROW), F32),
            vmem((4, FACE), jnp.int32),
            vmem((NB, TPR * TILE, 2 * TILE), BF16),
            vmem((NB, TPR * TILE, 2 * TILE), BF16),
            vmem((NB * LOADS, NB * TPR * LOADS), BF16),
            vmem((NB * LOADS, NB * TPR * LOADS), BF16),
            vmem((128, M), BF16),
            vmem((2 * DEFL, M), BF16),
            vmem((128, SLOTS), BF16),
            vmem((KROW, KROW), BF16),
            vmem((KROW, KROW), BF16),
            vmem((M, SLOTS), BF16),
            vmem((NB, wide, TILE), BF16),
            vmem((NB, wide, TILE), BF16),
            vmem((wide // 16, NB * TPR * LOADS, 2 * TILE), BF16),
            vmem((NB, 2 * LOADS, TILE), BF16),
            vmem((NB, 2 * LOADS, TILE), BF16),
            vmem((1, NB * TPR * LOADS, 2 * TILE), BF16),
            *[vmem((LOADS, M), F32)] * 6,
            *[vmem((LOADS, SLOTS), F32)] * 5,
            *[vmem((LOADS, 128), F32)] * 5,
            vmem((ITERS + 1, GRID, LOADS, 128), F32),
            vmem((GRID, LOADS, 128), F32),
            vmem((ITERS + 1, GRID, LOADS, 128), F32),
            vmem((4, LOADS, FACE), F32),
            vmem((ITERS, 4, LOADS, FACE), F32),
            dma((12,)),
            dma,
            dma,
            dma,
            dma((ITERS + 1,)),
            dma,
            dma((ITERS + 1,)),
            dma((4,)),
            dma((ITERS, 4)),
        ],
        compiler_params=pltpu.CompilerParams(
            collective_id=0, has_side_effects=True, vmem_limit_bytes=66_500_000
        ),
        name="feti",
    )(rhs, flex, flex_cols.T, stiff, stiff_cols.T, defl, coarse, face_rows, face_len)
    return pl.pallas_call(
        publish,
        out_shape=(field, field, field),
        in_specs=[vector, vector, vector],
        out_specs=(vector, vector, vector),
        compiler_params=pltpu.CompilerParams(vmem_limit_bytes=66_500_000),
        name="publish",
    )(*found)


def solution(mesh):
    return jax.shard_map(
        shards,
        mesh=mesh,
        in_specs=(
            P("row", "col"),
            P("row", "col"),
            P("row", "col"),
            P("row", "col"),
            P("row", "col"),
            P("row", "col"),
            P(("row", "col"), None),
            P("row", "col"),
            P("row", "col"),
        ),
        out_specs=(P("row", "col"), P("row", "col"), P("row", "col")),
        check_vma=False,
    )
```

time: 89.3 us -> 76.1 us (0.85)
  local copies, waits for them, and re-layouts: 7.13 us -> 0 us
  Pallas kernels: 81.2 us -> 75.3 us
    pallas_call x1, Pallas kernels: 81.2 us -> 73.7 us  [shards(): pl.pallas_call(kernel, out_shape=(field, field, field), in_specs=[anywher...]
    unnamed x5 -> x0, local copies, waits for them, and re-layouts: 7.13 us -> none
    pallas_call x0 -> x1, Pallas kernels: none -> 1.58 us  [shards(): pl.pallas_call(publish, out_shape=(field, field, field), in_specs=[vector...]
where the time goes in v2:
time: 76.1 us; the launch traced here: 75.9 us
  Pallas kernels  75.3 us (99%)
    pallas_call x1, Pallas kernels, shards(): pl.pallas_call(kernel, out_shape=(field, field, field), in_specs=[anywher...  73.7 us
    pallas_call x1, Pallas kernels, shards(): pl.pallas_call(publish, out_shape=(field, field, field), in_specs=[vector...  1.58 us

profile of v2, /device:TPU:1, one launch (start us, length us, event | category | flops | bytes accessed | tf_op | source)
XLA Modules:
  0.0 75.9 jit_solution(12407013462420550594)
XLA Ops:
  0.6 73.7 %feti.1 = (f32[8,2048]{1,0:T(8,128)}, f32[8,2048]{1,0:T(8,128)}, f32[8,2048]{1,0:T(8,128)}) custom-call(f32[8,2048]{1,0:T(8,128)} %rhs.1, f32[8192,128]{1,0:T(8,128)} %flex.1, s32[4,16]{1,0:T(4,128)} %bitcast.2, f32[8192,128]{1,0:T(8,128)} %stiff.1, s32[4,16]{1,0:T(4,128)} %bitcast.3, f32[32,2048]{1,0:T(8,128)} %defl.1, f32[32,8192]{1,0:T(8,128)} %coarse.1, ...), custom_call_target="tpu_custom_call" | custom-call | tf_op jit(solution)/shard_map/feti/pallas_call | solution.py:500
  74.3 1.6 %publish.1 = (f32[8,2048]{1,0:T(8,128)}, f32[8,2048]{1,0:T(8,128)}, f32[8,2048]{1,0:T(8,128)}) custom-call(f32[8,2048]{1,0:T(8,128)} %get-tuple-element.6.x_in, f32[8,2048]{1,0:T(8,128)} %get-tuple-element.7.r_in, f32[8,2048]{1,0:T(8,128)} %get-tuple-element.8.z_in), custom_call_target="tpu_custom_call" | custom-call | tf_op jit(solution)/shard_map/publish/pallas_call | solution.py:552

commit v3 on v2

--- a/solution.py
+++ b/solution.py
@@ -49,19 +49,32 @@
     return lax.broadcasted_iota(jnp.int32, shape, 0)
 
 
+def row_sum(value):
+    return jnp.sum(value, axis=1, keepdims=True)
+
+
+def turn(value, place):
+    moved = value
+    for groups in range(1, 4):
+        moved = jnp.where(place == groups, pltpu.roll(value, groups * DEFL, 1), moved)
+    return moved
+
+
 def kernel(
     rhs, flex, flex_cols, stiff, stiff_cols, defl, coarse, face_rows, face_len,
     x_ref, r_ref, z_ref,
     flex_f, stiff_f, defl_f, coarse_f, faces,
-    flex_t, stiff_t, flex_s, stiff_s, defl_t, image_t, trace_t, coarse_h, coarse_l, pick,
+    flex_t, stiff_t, flex_s, stiff_s, defl_t, image_t, trace_t, coarse_h, coarse_l, pick, couple_t,
     wide_a, wide_b, wide_spread, blocks_a, blocks_b, spread,
-    a_ref, b_ref, bw_ref, p_ref, q_ref, w_ref, tr_r, tr_z, tr_w, tr_p, tr_q,
-    e_r, e_q, s1_ref, alpha_ref, beta_ref,
-    recv1, send2, recv2, halo_out, halo_in,
-    load_sem, wsend, wrecv, send1_sem, recv1_sem, send2_sem, recv2_sem, hsend_sem, hrecv_sem,
+    a_ref, b_ref, bw_ref, p_ref, q_ref, w_ref, tr_r, tr_w, tr_q, jump_r, jump_w, jump_q,
+    e_r, e_q, s1_ref, alpha_ref, beta_ref, gr_ref, gq_ref, gw_ref, own_ref, c_ref, cq_ref,
+    row_g, recv1, send2, recv2, first_out, first_in, halo_out, halo_in,
+    load_sem, wsend, wrecv, send1_sem, recv1_sem, send2_sem, recv2_sem, fsend_sem, frecv_sem,
+    hsend_sem, hrecv_sem,
 ):
     i = lax.axis_index("row")
     j = lax.axis_index("col")
+    place = j % 4
     chunk = NB * TPR * TILE // 4
 
     def part_of(ref, index):
@@ -79,8 +92,6 @@
     load_stiff = [
         pltpu.make_async_copy(part_of(stiff, n), part_of(stiff_f, n), load_sem.at[8 + n]) for n in range(4)
     ]
-    for load in [load_r, load_z, load_faces] + load_flex + load_stiff + [load_coarse]:
-        load.start()
 
     row_partners = []
     for dy, dx in sorted(
@@ -92,12 +103,15 @@
         (j + offset) % GRID for offset in sorted(range(1, GRID), key=lambda o: -min(o, GRID - o))
     ]
 
+    load_r.start()
+    load_z.start()
     barrier = pltpu.get_barrier_semaphore()
     for there in row_partners:
         pl.semaphore_signal(barrier, inc=1, device_id=(there, j), device_id_type=MESH)
     for there in col_partners:
         pl.semaphore_signal(barrier, inc=1, device_id=(i, there), device_id_type=MESH)
-    pl.semaphore_wait(barrier, 2 * (GRID - 1))
+    for load in [load_faces] + load_flex + load_stiff + [load_coarse]:
+        load.start()
 
     def coarse_copy(there, slot):
         return pltpu.make_async_remote_copy(
@@ -109,10 +123,8 @@
             device_id_type=MESH,
         )
 
-    for there in row_partners:
-        coarse_copy(there, i).start()
-
     lane8 = lane_ids((LOADS, 128))
+    group8 = lane8 // DEFL
 
     def copy1(phase, there):
         return pltpu.make_async_remote_copy(
@@ -166,57 +178,78 @@
             device_id_type=MESH,
         )
 
-    def gather_start(phase, coefficients, sums):
-        payload = jnp.where(lane8 < DEFL, coefficients, 0.0)
-        for place, value in enumerate(sums):
-            payload = jnp.where(lane8 == DEFL + place, value, payload)
-        recv1[phase, j] = payload
+    def gather_start(phase, coefficients, energy, sums):
+        recv1[phase, j, 0:LOADS] = coefficients
+        second = jnp.where(group8 == 1, energy, 0.0)
+        for index, value in enumerate(sums):
+            second = jnp.where(lane8 == 3 * DEFL + index, value, second)
+        recv1[phase, j, LOADS : 2 * LOADS] = second
         for there in col_partners:
             copy1(phase, there).start()
 
     def gather_middle(phase, before_matmul=None):
         whole1(phase).wait_recv()
-        total = jnp.zeros((LOADS, 128), F32)
+        first = [recv1[phase, source, 0:LOADS] for source in range(GRID)]
         groups = []
-        for group in range(4):
+        for quarter in range(4):
             gathered = None
-            for place in range(4):
-                payload = recv1[phase, group * 4 + place]
-                total = total + payload
-                moved = jnp.where(lane8 < DEFL, payload, 0.0)
-                if place:
-                    moved = pltpu.roll(moved, place * DEFL, 1)
-                gathered = moved if gathered is None else gathered + moved
+            for offset in range(4):
+                source = quarter * 4 + offset
+                value = first[source]
+                if source:
+                    value = value + first[source - 1]
+                if source < GRID - 1:
+                    value = value + first[source + 1]
+                gathered = value if gathered is None else jnp.where(group8 == offset, value, gathered)
             groups.append(gathered)
         if before_matmul is not None:
             before_matmul()
         operand = parts(jnp.concatenate(groups, axis=1))
         partial = fold(dot_nt(operand, coarse_h[...]) + dot_nt(operand, coarse_l[...]))
-        total = jnp.where((lane8 >= DEFL) & (lane8 < 2 * DEFL), total, 0.0)
-        rolled = [total] + [pltpu.roll(total, place * DEFL, 1) for place in range(1, 4)]
+        total = None
+        crossed = None
+        for quarter in range(4):
+            energies = None
+            for offset in range(4):
+                second = recv1[phase, quarter * 4 + offset, LOADS : 2 * LOADS]
+                total = second if total is None else total + second
+                shift = ((offset + 3) % 4) * DEFL
+                moved = pltpu.roll(second, shift, 1) if shift else second
+                energies = moved if energies is None else jnp.where(group8 == offset, moved, energies)
+            crossed = groups[quarter] * energies + (0.0 if crossed is None else crossed)
+        total = total + jnp.where(lane8 == 3 * DEFL, row_sum(crossed), 0.0)
+        tiles = [partial[:, n * 128 : (n + 1) * 128] for n in range(4)]
+        turned = [
+            [tile if not n else pltpu.roll(tile, 128 - n * DEFL, 1) for n in range(4)] for tile in tiles
+        ]
         for target in range(GRID):
-            tile = partial[:, (target // 4) * 128 : (target // 4 + 1) * 128]
-            send2[target] = jnp.where(lane8 // DEFL == target % 4, tile, rolled[target % 4])
+            before = (target + GRID - 1) % GRID
+            quarter, offset = before // 4, before % 4
+            value = turned[quarter][offset]
+            if offset > 1:
+                value = jnp.where(group8 < 4 - offset, value, turned[(quarter + 1) % 4][offset])
+            send2[target] = jnp.where(group8 < 3, value, total)
         for there in row_partners:
             copy2(phase, there).start()
         recv2[phase, i] = send2[i]
+        for quarter in range(4):
+            row_g[quarter] = groups[quarter]
+        mine = jnp.where(group8 == place, row_g[j // 4], 0.0)
+        own_ref[...] = turn(mine, (5 - place) % 4)
 
     def gather_end(phase):
         whole2(phase).wait_recv()
         level = [recv2[phase, source] for source in range(GRID)]
         while len(level) > 1:
             level = [level[n] + level[n + 1] for n in range(0, len(level), 2)]
-        result = level[0]
-        turned = result
-        for place in range(1, 4):
-            turned = jnp.where(i % 4 == place, pltpu.roll(result, 128 - place * DEFL, 1), turned)
         whole1(phase).wait_send()
         whole2(phase).wait_send()
-        return turned
+        return level[0]
 
     def coefficients_of(product):
         summed = fold(product)
-        return summed + pltpu.roll(summed, 128 - DEFL, 1)
+        summed = summed + pltpu.roll(summed, 128 - DEFL, 1)
+        return jnp.where(lane8 < DEFL, summed, 0.0)
 
     load_r.wait()
     load_z.wait()
@@ -225,8 +258,63 @@
     defl_t[0:DEFL] = defl_high
     defl_t[DEFL : 2 * DEFL] = defl_low
     defl_t[2 * DEFL :] = jnp.zeros((128 - 2 * DEFL, M), BF16)
-    gather_start(0, coefficients_of(dot_nt(parts(r_ref[...]), defl_t[...])), ())
-
+    started = coefficients_of(dot_nt(parts(r_ref[...]), defl_t[...]))
+    c_ref[...] = pltpu.roll(started, DEFL, 1)
+    pl.semaphore_wait(barrier, 2 * (GRID - 1))
+    for there in row_partners:
+        coarse_copy(there, i).start()
+    gather_start(0, turn(started, place), jnp.zeros((LOADS, 128), F32), ())
+
+    sides = (
+        (i > 0, (i - 1, j), 1),
+        (i < GRID - 1, (i + 1, j), 0),
+        (j > 0, (i, j - 1), 3),
+        (j < GRID - 1, (i, j + 1), 2),
+    )
+
+    def first_copy(face, device, slot):
+        return pltpu.make_async_remote_copy(
+            src_ref=first_out.at[face],
+            dst_ref=first_in.at[slot],
+            send_sem=fsend_sem.at[face],
+            recv_sem=frecv_sem.at[slot],
+            device_id=device,
+            device_id_type=MESH,
+        )
+
+    def face_copy(step, kind, face, device, slot):
+        return pltpu.make_async_remote_copy(
+            src_ref=halo_out.at[kind, face],
+            dst_ref=halo_in.at[step, kind, slot],
+            send_sem=hsend_sem.at[kind, face],
+            recv_sem=hrecv_sem.at[step, kind, slot],
+            device_id=device,
+            device_id_type=MESH,
+        )
+
+    def send_faces(step, kind, traces):
+        for face in range(4):
+            halo_out[kind, face] = traces[:, face * FACE : (face + 1) * FACE]
+        for face, (inside, device, slot) in enumerate(sides):
+
+            @pl.when(inside)
+            def _():
+                face_copy(step, kind, face, device, slot).start()
+
+    def take_faces(step, kind, traces):
+        for face, (inside, device, slot) in enumerate(sides):
+
+            @pl.when(inside)
+            def _():
+                face_copy(step, kind, slot, device, face).wait_recv()
+                face_copy(step, kind, face, device, slot).wait_send()
+
+        partner = jnp.concatenate([halo_in[step, kind, face] for face in range(4)], axis=1)
+        return jnp.where(live > 0.5, traces - partner, 0.0)
+
+    live = jnp.concatenate(
+        [jnp.where(lane8 < face_len[0, face], 1.0, 0.0) for face in range(4)], axis=1
+    )
     load_faces.wait()
 
     def build_pick(block, carry):
@@ -246,6 +334,13 @@
     tr_r[...] = both[0:LOADS]
     trace_t[0 : 2 * DEFL] = parts(both[LOADS:])
     trace_t[2 * DEFL :] = jnp.zeros((128 - 2 * DEFL, SLOTS), BF16)
+    for face in range(4):
+        first_out[face] = both[:, face * FACE : (face + 1) * FACE]
+    for face, (inside, device, slot) in enumerate(sides):
+
+        @pl.when(inside)
+        def _():
+            first_copy(face, device, slot).start()
 
     def build_spread(columns, target):
         lanes = lane_ids((LOADS, 128))
@@ -253,9 +348,9 @@
         across = lane_ids((NB * LOADS, 128))
         for tile in range(4):
             named = jnp.zeros((LOADS, 128), jnp.int32)
-            for place in range(16):
-                index = tile * 16 + place
-                named = jnp.where(lanes // LOADS == place, columns[index % TPR, index // TPR], named)
+            for spot in range(16):
+                index = tile * 16 + spot
+                named = jnp.where(lanes // LOADS == spot, columns[index % TPR, index // TPR], named)
             hit = (rows // LOADS == named[0:1, :]) & (rows % LOADS == across % LOADS)
             target[:, tile * 128 : (tile + 1) * 128] = jnp.where(hit, 1.0, 0.0).astype(BF16)
 
@@ -329,48 +424,85 @@
         wide_b[block] = parts(middle[block])
     applied = backward(wide_b, flex_t, flex_s, wide_spread)
     for block in range(NB):
-        cut = slice(block * TILE, (block + 1) * TILE)
-        a_ref[:, cut] = r_ref[:, cut] + applied[block][0:LOADS]
-        image_t[:, cut] = parts(defl_f[:, cut] + applied[block][LOADS:wide])
+        span = slice(block * TILE, (block + 1) * TILE)
+        a_ref[:, span] = r_ref[:, span] + applied[block][0:LOADS]
+        image_t[:, span] = parts(defl_f[:, span] + applied[block][LOADS:wide])
+
+    for face, (inside, device, slot) in enumerate(sides):
+
+        @pl.when(inside)
+        def _():
+            first_copy(slot, device, face).wait_recv()
+            first_copy(face, device, slot).wait_send()
+
+    def operator_coefficients(field, jump):
+        return coefficients_of(dot_nt(parts(field), defl_t[...]) + dot_nt(parts(jump), trace_t[...]))
+
+    partner = jnp.concatenate([first_in[face, 0:LOADS] for face in range(4)], axis=1)
+    jump = jnp.where(live > 0.5, tr_r[...] - partner, 0.0)
+    jump_r[...] = jump
+    found = operator_coefficients(a_ref[...], jump)
+    gr_ref[0] = turn(found, place)
+    gr_ref[1] = pltpu.roll(found, DEFL, 1)
+
+    traces = [first_out[face, LOADS:wide] for face in range(4)]
+    others = [
+        jnp.where(live[0:1, face * FACE : (face + 1) * FACE] > 0.5, first_in[face, LOADS:wide], 0.0)
+        for face in range(4)
+    ]
+    masked = [
+        jnp.where(live[0:1, face * FACE : (face + 1) * FACE] > 0.5, traces[face], 0.0)
+        for face in range(4)
+    ]
+    lane32 = lane_ids((DEFL, 128))
+
+    def paired(product):
+        summed = fold(product)
+        summed = summed + pltpu.roll(summed, 128 - DEFL, 1)
+        return jnp.where(lane32 < DEFL, summed, 0.0)
+
+    def against(value):
+        return jnp.concatenate([parts(value), jnp.zeros((2 * DEFL, FACE), BF16)], axis=0)
+
+    own = dot_nt(image_t[...], defl_t[...])
+    for face in range(4):
+        own = own + dot_nt(parts(masked[face]), trace_t[:, face * FACE : (face + 1) * FACE])
+    north = paired(dot_nt(parts(others[0]), trace_t[:, 0:FACE]))
+    south = paired(dot_nt(parts(others[1]), trace_t[:, FACE : 2 * FACE]))
+    west = paired(dot_nt(parts(masked[2]), against(others[2])))
+    east = paired(dot_nt(parts(masked[3]), against(others[3])))
+    couple = jnp.concatenate(
+        [
+            -turn(north, place),
+            turn(paired(own), place) - turn(west, (place + 3) % 4) - turn(east, (place + 1) % 4),
+            -turn(south, place),
+            jnp.zeros((DEFL, 128), F32),
+        ],
+        axis=0,
+    )
+    couple_t[...] = parts(couple)
 
     zeros = jnp.zeros((LOADS, M), F32)
     for ref in (b_ref, bw_ref, p_ref, q_ref, w_ref, x_ref, z_ref):
         ref[...] = zeros
-    tr_p[...] = jnp.zeros((LOADS, SLOTS), F32)
-    tr_q[...] = jnp.zeros((LOADS, SLOTS), F32)
-    tr_z[...] = jnp.zeros((LOADS, SLOTS), F32)
-    e_q[...] = jnp.zeros((LOADS, 128), F32)
+    short = jnp.zeros((LOADS, SLOTS), F32)
+    for ref in (tr_w, tr_q, jump_w, jump_q):
+        ref[...] = short
+    none = jnp.zeros((LOADS, 128), F32)
+    for ref in (e_q, alpha_ref, beta_ref, cq_ref):
+        ref[...] = none
+    for layout in range(2):
+        gq_ref[layout] = none
+        gw_ref[layout] = none
     s1_ref[...] = jnp.ones((LOADS, 128), F32)
-    alpha_ref[...] = jnp.zeros((LOADS, 128), F32)
-    beta_ref[...] = jnp.zeros((LOADS, 128), F32)
-
-    e_r[...] = jnp.where(lane8 < DEFL, gather_end(0), 0.0)
+
+    e_r[...] = jnp.where(group8 < 3, gather_end(0), 0.0)
+    own_ref[...] = none
     whole_coarse().wait_send()
 
     def energy_parts():
-        energy = e_r[...]
-        return parts(energy + pltpu.roll(energy, DEFL, 1))[:, 0 : 2 * DEFL]
-
-    def face_copy(step, face, device, slot):
-        return pltpu.make_async_remote_copy(
-            src_ref=halo_out.at[face],
-            dst_ref=halo_in.at[step, slot],
-            send_sem=hsend_sem.at[face],
-            recv_sem=hrecv_sem.at[step, slot],
-            device_id=device,
-            device_id_type=MESH,
-        )
-
-    sides = (
-        (i > 0, (i - 1, j), 1),
-        (i < GRID - 1, (i + 1, j), 0),
-        (j > 0, (i, j - 1), 3),
-        (j < GRID - 1, (i, j + 1), 2),
-    )
-
-    live = jnp.concatenate(
-        [jnp.where(lane8 < face_len[0, face], 1.0, 0.0) for face in range(4)], axis=1
-    )
+        energy = jnp.where(group8 == 1, e_r[...], 0.0)
+        return parts(energy + pltpu.roll(energy, 128 - DEFL, 1))[:, 0 : 2 * DEFL]
 
     def advance():
         alpha = alpha_ref[:, 0:1]
@@ -379,108 +511,100 @@
         image = w_ref[...] + beta * q_ref[...]
         p_ref[...] = direction
         q_ref[...] = image
-        x_ref[...] = x_ref[...] + alpha * direction
         residual = r_ref[...] - alpha * image
         r_ref[...] = residual
         return alpha, beta, direction, image, residual
 
-    def row_sum(value):
-        return jnp.sum(value, axis=1, keepdims=True)
-
     def iterate(step, carry):
-        energy = energy_parts()
-        old_traces = tr_z[...]
-        traces = tr_r[...] + fold(dot_nn(energy, trace_t[0 : 2 * DEFL]))
-        tr_z[...] = traces
-        for face in range(4):
-            halo_out[face] = traces[:, face * FACE : (face + 1) * FACE]
-        for face, (inside, device, slot) in enumerate(sides):
-
-            @pl.when(inside)
-            def _():
-                face_copy(step, face, device, slot).start()
-
+        energies = e_r[...]
+        doubled = parts(energies)
+        coefficients = fold(dot_nn(jnp.concatenate([doubled, doubled], axis=1), couple_t[...]))
         alpha, beta, p, q, r = advance()
-        tr_p[...] = old_traces + beta * tr_p[...]
         applied = bw_ref[...] + beta * b_ref[...]
         b_ref[...] = applied
         a = a_ref[...] - alpha * applied
         a_ref[...] = a
-        z = r + fold(dot_nn(energy, defl_t[0 : 2 * DEFL]))
-        z_ref[...] = z
-        u = a + fold(dot_nn(energy, image_t[...]))
-        w_ref[...] = u
-        product = dot_nt(parts(u), defl_t[...])
-        sum_zu = row_sum(z * u)
-        sum_pu = row_sum(p * u)
-        sum_rz = row_sum(r * z)
+        for layout in range(2):
+            image = gw_ref[layout] + beta * gq_ref[layout]
+            gq_ref[layout] = image
+            gr_ref[layout] = gr_ref[layout] - alpha * image
+        image = own_ref[...] + beta * cq_ref[...]
+        cq_ref[...] = image
+        c = c_ref[...] - alpha * image
+        c_ref[...] = c
+        trace_q = tr_w[...] + beta * tr_q[...]
+        tr_q[...] = trace_q
+        tr = tr_r[...] - alpha * trace_q
+        tr_r[...] = tr
+        jump_q_now = jump_w[...] + beta * jump_q[...]
+        jump_q[...] = jump_q_now
+        jump_now = jump_r[...] - alpha * jump_q_now
+        jump_r[...] = jump_now
+        sum_zar = row_sum(r * a) + row_sum(tr * jump_now) + row_sum(energies * gr_ref[1])
+        sum_rz = row_sum(r * r) + row_sum(energies * c)
         sum_rp = row_sum(r * p)
-        sum_zq = row_sum(z * q)
-
-        for face, (inside, device, slot) in enumerate(sides):
-
-            @pl.when(inside)
-            def _():
-                face_copy(step, slot, device, face).wait_recv()
-
-        partner = jnp.concatenate([halo_in[step, face] for face in range(4)], axis=1)
-        jump = jnp.where(live > 0.5, tr_z[...] - partner, 0.0)
-        jump_parts = parts(jump)
-        product = product + dot_nt(jump_parts, trace_t[...])
-        sum_zw = sum_zu + row_sum(tr_z[...] * jump)
-        sum_pw = sum_pu + row_sum(tr_p[...] * jump)
-        gather_start(step + 1, coefficients_of(product), (sum_zw, sum_pw, sum_rz, sum_rp, sum_zq))
-
-        w = w_ref[...] + fold(dot_nt(jump_parts, pick[...]))
+        sum_zq = row_sum(r * q) + row_sum(energies * image)
+        gather_start(
+            step + 1, coefficients + gr_ref[0], energies, (sum_zar, sum_rz, sum_rp, sum_zq)
+        )
+
+        energy = energy_parts()
+        traces = tr + fold(dot_nn(energy, trace_t[0 : 2 * DEFL]))
+        send_faces(step, 0, traces)
+        x_ref[...] = x_ref[...] + alpha * p
+        z_ref[...] = r_ref[...] + fold(dot_nn(energy, defl_t[0 : 2 * DEFL]))
+        w_ref[...] = a_ref[...] + fold(dot_nn(energy, image_t[...]))
+        jump = take_faces(step, 0, traces)
+        w = w_ref[...] + fold(dot_nt(parts(jump), pick[...]))
         w_ref[...] = w
         split = parts(w)
         for block in range(NB):
             blocks_a[block] = split[:, block * TILE : (block + 1) * TILE]
-        for face, (inside, device, slot) in enumerate(sides):
-
-            @pl.when(inside)
-            def _():
-                face_copy(step, face, device, slot).wait_send()
 
         @pl.when(step < ITERS - 1)
         def _():
-            tr_w[...] = fold(dot_nn(split, pick[...]))
-            forward(blocks_a, flex_t, flex_cols, blocks_b)
+            image = fold(dot_nn(split, pick[...]))
+            tr_w[...] = image
+            send_faces(step, 1, image)
 
         gather_middle(step + 1)
 
         @pl.when(step < ITERS - 1)
         def _():
+            forward(blocks_a, flex_t, flex_cols, blocks_b)
             forward(blocks_b, stiff_t, stiff_cols, blocks_a)
             middle = backward(blocks_a, stiff_t, stiff_s, spread)
             for block in range(NB):
                 blocks_b[block] = parts(middle[block])
             local = backward(blocks_b, flex_t, flex_s, spread)
-            bw_ref[...] = w_ref[...] + jnp.concatenate(local, axis=1)
+            image = w_ref[...] + jnp.concatenate(local, axis=1)
+            bw_ref[...] = image
+            jump = take_faces(step, 1, tr_w[...])
+            jump_w[...] = jump
+            found = operator_coefficients(image, jump)
+            gw_ref[0] = turn(found, place)
+            gw_ref[1] = pltpu.roll(found, DEFL, 1)
 
         gathered = gather_end(step + 1)
 
-        def total(place):
-            return gathered[:, DEFL + place : DEFL + place + 1]
-
-        new_beta = -total(4) / s1_ref[:, 0:1]
-        curvature = total(0) + new_beta * total(1)
-        new_alpha = (total(2) + new_beta * total(3)) / curvature
+        def total(index):
+            return gathered[:, 3 * DEFL + index : 3 * DEFL + index + 1]
+
+        new_beta = -total(3) / s1_ref[:, 0:1]
+        curvature = total(0) + new_beta * total(3)
+        new_alpha = (total(1) + new_beta * total(2)) / curvature
         s1_ref[...] = jnp.broadcast_to(curvature, (LOADS, 128))
         alpha_ref[...] = jnp.broadcast_to(new_alpha, (LOADS, 128))
         beta_ref[...] = jnp.broadcast_to(new_beta, (LOADS, 128))
-        energy_q = jnp.where(lane8 < DEFL, gathered, 0.0) + new_beta * e_q[...]
+        energy_q = jnp.where(group8 < 3, gathered, 0.0) + new_beta * e_q[...]
         e_q[...] = energy_q
         e_r[...] = e_r[...] - new_alpha * energy_q
-        trace_q = tr_w[...] + new_beta * tr_q[...]
-        tr_q[...] = trace_q
-        tr_r[...] = tr_r[...] - new_alpha * trace_q
         return carry
 
-    tr_w[...] = jnp.zeros((LOADS, SLOTS), F32)
     lax.fori_loop(0, ITERS, iterate, 0)
-    advance()
-    z_ref[...] = r_ref[...] + fold(dot_nn(energy_parts(), defl_t[0 : 2 * DEFL]))
+    alpha, _, p, _, r = advance()
+    x_ref[...] = x_ref[...] + alpha * p
+    z_ref[...] = r + fold(dot_nn(energy_parts(), defl_t[0 : 2 * DEFL]))
 
 
 def publish(x_in, r_in, z_in, x_out, r_out, z_out):
@@ -520,6 +644,7 @@
             vmem((KROW, KROW), BF16),
             vmem((KROW, KROW), BF16),
             vmem((M, SLOTS), BF16),
+            vmem((256, 128), BF16),
             vmem((NB, wide, TILE), BF16),
             vmem((NB, wide, TILE), BF16),
             vmem((wide // 16, NB * TPR * LOADS, 2 * TILE), BF16),
@@ -527,13 +652,18 @@
             vmem((NB, 2 * LOADS, TILE), BF16),
             vmem((1, NB * TPR * LOADS, 2 * TILE), BF16),
             *[vmem((LOADS, M), F32)] * 6,
-            *[vmem((LOADS, SLOTS), F32)] * 5,
+            *[vmem((LOADS, SLOTS), F32)] * 6,
             *[vmem((LOADS, 128), F32)] * 5,
-            vmem((ITERS + 1, GRID, LOADS, 128), F32),
+            *[vmem((2, LOADS, 128), F32)] * 3,
+            *[vmem((LOADS, 128), F32)] * 3,
+            vmem((4, LOADS, 128), F32),
+            vmem((ITERS + 1, GRID, 2 * LOADS, 128), F32),
             vmem((GRID, LOADS, 128), F32),
             vmem((ITERS + 1, GRID, LOADS, 128), F32),
-            vmem((4, LOADS, FACE), F32),
-            vmem((ITERS, 4, LOADS, FACE), F32),
+            vmem((4, LOADS + DEFL, FACE), F32),
+            vmem((4, LOADS + DEFL, FACE), F32),
+            vmem((2, 4, LOADS, FACE), F32),
+            vmem((ITERS, 2, 4, LOADS, FACE), F32),
             dma((12,)),
             dma,
             dma,
@@ -542,7 +672,9 @@
             dma,
             dma((ITERS + 1,)),
             dma((4,)),
-            dma((ITERS, 4)),
+            dma((4,)),
+            dma((2, 4)),
+            dma((ITERS, 2, 4)),
         ],
         compiler_params=pltpu.CompilerParams(
             collective_id=0, has_side_effects=True, vmem_limit_bytes=66_500_000

time: 76.1 us -> 67.8 us (0.89)
  Pallas kernels: 75.3 us -> 67 us
    pallas_call x1, Pallas kernels: 73.7 us -> 65.4 us  [shards(): pl.pallas_call(kernel, out_shape=(field, field, field), in_specs=[anywher...]
where the time goes in v3:
time: 67.8 us; the launch traced here: 67.6 us
  Pallas kernels  67 us (99%)
    pallas_call x1, Pallas kernels, shards(): pl.pallas_call(kernel, out_shape=(field, field, field), in_specs=[anywher...  65.4 us
    pallas_call x1, Pallas kernels, shards(): pl.pallas_call(publish, out_shape=(field, field, field), in_specs=[vector...  1.58 us

profile of v3, /device:TPU:1, one launch (start us, length us, event | category | flops | bytes accessed | tf_op | source)
XLA Modules:
  0.0 67.6 jit_solution(13245502126696005603)
XLA Ops:
  0.6 65.4 %feti.1 = (f32[8,2048]{1,0:T(8,128)}, f32[8,2048]{1,0:T(8,128)}, f32[8,2048]{1,0:T(8,128)}) custom-call(f32[8,2048]{1,0:T(8,128)} %rhs.1, f32[8192,128]{1,0:T(8,128)} %flex.1, s32[4,16]{1,0:T(4,128)} %bitcast.2, f32[8192,128]{1,0:T(8,128)} %stiff.1, s32[4,16]{1,0:T(4,128)} %bitcast.3, f32[32,2048]{1,0:T(8,128)} %defl.1, f32[32,8192]{1,0:T(8,128)} %coarse.1, ...), custom_call_target="tpu_custom_call" | custom-call | tf_op jit(solution)/shard_map/feti/pallas_call | solution.py:624
  66.0 1.6 %publish.1 = (f32[8,2048]{1,0:T(8,128)}, f32[8,2048]{1,0:T(8,128)}, f32[8,2048]{1,0:T(8,128)}) custom-call(f32[8,2048]{1,0:T(8,128)} %get-tuple-element.6.x_in, f32[8,2048]{1,0:T(8,128)} %get-tuple-element.7.r_in, f32[8,2048]{1,0:T(8,128)} %get-tuple-element.8.z_in), custom_call_target="tpu_custom_call" | custom-call | tf_op jit(solution)/shard_map/publish/pallas_call | solution.py:684

commit v4 on v3

--- a/solution.py
+++ b/solution.py
@@ -63,18 +63,22 @@
 def kernel(
     rhs, flex, flex_cols, stiff, stiff_cols, defl, coarse, face_rows, face_len,
     x_ref, r_ref, z_ref,
-    flex_f, stiff_f, defl_f, coarse_f, faces,
-    flex_t, stiff_t, flex_s, stiff_s, defl_t, image_t, trace_t, coarse_h, coarse_l, pick, couple_t,
+    flex_f, stiff_f, defl_f, coarse_own, coarse_f, across_out, across_in, faces,
+    flex_t, stiff_t, flex_s, stiff_s, defl_t, image_t, trace_t, coarse_h, coarse_l, across_h, across_l, pick, couple_t,
     wide_a, wide_b, wide_spread, blocks_a, blocks_b, spread,
     a_ref, b_ref, bw_ref, p_ref, q_ref, w_ref, tr_r, tr_w, tr_q, jump_r, jump_w, jump_q,
     e_r, e_q, s1_ref, alpha_ref, beta_ref, gr_ref, gq_ref, gw_ref, own_ref, c_ref, cq_ref,
     row_g, recv1, send2, recv2, first_out, first_in, halo_out, halo_in,
-    load_sem, wsend, wrecv, send1_sem, recv1_sem, send2_sem, recv2_sem, fsend_sem, frecv_sem,
+    load_sem, wsend, wrecv, asend, arecv, send1_sem, recv1_sem, send2_sem, recv2_sem, fsend_sem, frecv_sem,
     hsend_sem, hrecv_sem,
 ):
     i = lax.axis_index("row")
     j = lax.axis_index("col")
     place = j % 4
+    pair = j // 4
+    odd = (j // 2) % 2
+    beside = (pair + 3 + 2 * odd) % 4
+    far_groups = ((pair + 2) % 4, (pair + 1 + 2 * odd) % 4)
     chunk = NB * TPR * TILE // 4
 
     def part_of(ref, index):
@@ -83,9 +87,7 @@
     load_r = pltpu.make_async_copy(rhs, r_ref, load_sem.at[0])
     load_z = pltpu.make_async_copy(defl, defl_f, load_sem.at[1])
     load_faces = pltpu.make_async_copy(face_rows, faces, load_sem.at[2])
-    load_coarse = pltpu.make_async_copy(
-        coarse.at[:, pl.ds(pl.multiple_of(i * KROW, KROW), KROW)], coarse_f.at[i], load_sem.at[3]
-    )
+    load_coarse = pltpu.make_async_copy(coarse, coarse_own, load_sem.at[3])
     load_flex = [
         pltpu.make_async_copy(part_of(flex, n), part_of(flex_f, n), load_sem.at[4 + n]) for n in range(4)
     ]
@@ -110,13 +112,16 @@
         pl.semaphore_signal(barrier, inc=1, device_id=(there, j), device_id_type=MESH)
     for there in col_partners:
         pl.semaphore_signal(barrier, inc=1, device_id=(i, there), device_id_type=MESH)
-    for load in [load_faces] + load_flex + load_stiff + [load_coarse]:
+    for load in [load_coarse, load_faces] + load_flex + load_stiff:
         load.start()
 
-    def coarse_copy(there, slot):
-        return pltpu.make_async_remote_copy(
-            src_ref=coarse.at[:, pl.ds(pl.multiple_of(there * KROW, KROW), KROW)],
-            dst_ref=coarse_f.at[slot],
+    def coarse_lanes(row, group):
+        return pl.ds(pl.multiple_of(row * KROW + group * 128, 128), 128)
+
+    def coarse_copy(there, part):
+        return pltpu.make_async_remote_copy(
+            src_ref=coarse.at[:, coarse_lanes(there, far_groups[part])],
+            dst_ref=coarse_f.at[i, part],
             send_sem=wsend,
             recv_sem=wrecv,
             device_id=(there, j),
@@ -163,6 +168,26 @@
             dst_ref=recv2.at[phase, pl.ds(0, GRID - 1)],
             send_sem=send2_sem,
             recv_sem=recv2_sem.at[phase],
+            device_id=(i, j),
+            device_id_type=MESH,
+        )
+
+    def across_copy(piece, there, slot):
+        return pltpu.make_async_remote_copy(
+            src_ref=across_out.at[piece],
+            dst_ref=across_in.at[slot],
+            send_sem=asend,
+            recv_sem=arecv,
+            device_id=(i, there),
+            device_id_type=MESH,
+        )
+
+    def whole_across():
+        return pltpu.make_async_remote_copy(
+            src_ref=across_out.at[pl.ds(0, 7)],
+            dst_ref=across_in.at[pl.ds(0, 7)],
+            send_sem=asend,
+            recv_sem=arecv,
             device_id=(i, j),
             device_id_type=MESH,
         )
@@ -204,8 +229,16 @@
             groups.append(gathered)
         if before_matmul is not None:
             before_matmul()
-        operand = parts(jnp.concatenate(groups, axis=1))
-        partial = fold(dot_nt(operand, coarse_h[...]) + dot_nt(operand, coarse_l[...]))
+        for quarter in range(4):
+            row_g[quarter] = groups[quarter]
+        near = parts(jnp.concatenate([row_g[pair], row_g[beside]], axis=1))
+        far = parts(jnp.concatenate([row_g[far_groups[0]], row_g[far_groups[1]]], axis=1))
+        partial = fold(
+            dot_nn(near, across_h[...])
+            + dot_nn(near, across_l[...])
+            + dot_nt(far, coarse_h[...])
+            + dot_nt(far, coarse_l[...])
+        )
         total = None
         crossed = None
         for quarter in range(4):
@@ -232,8 +265,6 @@
         for there in row_partners:
             copy2(phase, there).start()
         recv2[phase, i] = send2[i]
-        for quarter in range(4):
-            row_g[quarter] = groups[quarter]
         mine = jnp.where(group8 == place, row_g[j // 4], 0.0)
         own_ref[...] = turn(mine, (5 - place) % 4)
 
@@ -262,8 +293,33 @@
     c_ref[...] = pltpu.roll(started, DEFL, 1)
     pl.semaphore_wait(barrier, 2 * (GRID - 1))
     for there in row_partners:
-        coarse_copy(there, i).start()
+        for part in range(2):
+            coarse_copy(there, part).start()
     gather_start(0, turn(started, place), jnp.zeros((LOADS, 128), F32), ())
+
+    load_coarse.wait()
+    group32 = lane_ids((DEFL, 128)) // DEFL
+    after, ahead = (pair + 1) % 4, (pair + 3) % 4
+    for piece, (group, spot) in enumerate(
+        [(pair, 0), (pair, 1), (pair, 2), (pair, 3), (after, 0), (after, 1), (ahead, 2), (ahead, 3)]
+    ):
+        for quarter in range(4):
+            packed = None
+            for offset in range(4):
+                value = coarse_own[:, coarse_lanes(quarter * 4 + offset, group)]
+                shift = ((offset - spot) % 4) * DEFL
+                if shift:
+                    value = pltpu.roll(value, shift, 1)
+                packed = value if packed is None else jnp.where(group32 == offset, value, packed)
+            across_out[piece, :, quarter * 128 : (quarter + 1) * 128] = packed
+    for piece, there in ((4, after * 4), (5, after * 4 + 1), (6, ahead * 4 + 2), (7, ahead * 4 + 3)):
+        across_copy(piece, there, 4 + place).start()
+    for step in range(1, 4):
+        other = (place + step) % 4
+        across_copy(other, pair * 4 + other, place).start()
+    across_in[place] = across_out[place]
+    for part in range(2):
+        coarse_f[i, part] = coarse_own[:, coarse_lanes(i, far_groups[part])]
 
     sides = (
         (i > 0, (i - 1, j), 1),
@@ -292,9 +348,11 @@
             device_id_type=MESH,
         )
 
-    def send_faces(step, kind, traces):
+    def store_faces(kind, traces):
         for face in range(4):
             halo_out[kind, face] = traces[:, face * FACE : (face + 1) * FACE]
+
+    def start_faces(step, kind):
         for face, (inside, device, slot) in enumerate(sides):
 
             @pl.when(inside)
@@ -374,15 +432,27 @@
     convert(load_stiff, stiff_f, stiff_t)
 
     def coarse_ready():
-        load_coarse.wait()
-        whole_coarse().wait_recv()
-
-        def one(block, carry):
-            rows = coarse_f[block]
+        whole_across().wait_recv()
+
+        def one_across(block, carry):
+            rows = across_in[block]
             high = rows.astype(BF16)
             start = pl.multiple_of(block * DEFL, DEFL)
-            coarse_h[pl.ds(start, DEFL), :] = high
-            coarse_l[pl.ds(start, DEFL), :] = (rows - high.astype(F32)).astype(BF16)
+            across_h[pl.ds(start, DEFL), :] = high
+            across_l[pl.ds(start, DEFL), :] = (rows - high.astype(F32)).astype(BF16)
+            return carry
+
+        lax.fori_loop(0, 8, one_across, 0)
+        whole_coarse().wait_recv()
+
+        def one(block, carry):
+            start = pl.multiple_of(block * DEFL, DEFL)
+            for part in range(2):
+                rows = coarse_f[block, part]
+                high = rows.astype(BF16)
+                lanes = slice(part * 128, (part + 1) * 128)
+                coarse_h[pl.ds(start, DEFL), lanes] = high
+                coarse_l[pl.ds(start, DEFL), lanes] = (rows - high.astype(F32)).astype(BF16)
             return carry
 
         lax.fori_loop(0, GRID, one, 0)
@@ -499,6 +569,7 @@
     e_r[...] = jnp.where(group8 < 3, gather_end(0), 0.0)
     own_ref[...] = none
     whole_coarse().wait_send()
+    whole_across().wait_send()
 
     def energy_parts():
         energy = jnp.where(group8 == 1, e_r[...], 0.0)
@@ -544,13 +615,14 @@
         sum_rz = row_sum(r * r) + row_sum(energies * c)
         sum_rp = row_sum(r * p)
         sum_zq = row_sum(r * q) + row_sum(energies * image)
+        energy = energy_parts()
+        traces = tr + fold(dot_nn(energy, trace_t[0 : 2 * DEFL]))
+        store_faces(0, traces)
         gather_start(
             step + 1, coefficients + gr_ref[0], energies, (sum_zar, sum_rz, sum_rp, sum_zq)
         )
 
-        energy = energy_parts()
-        traces = tr + fold(dot_nn(energy, trace_t[0 : 2 * DEFL]))
-        send_faces(step, 0, traces)
+        start_faces(step, 0)
         x_ref[...] = x_ref[...] + alpha * p
         z_ref[...] = r_ref[...] + fold(dot_nn(energy, defl_t[0 : 2 * DEFL]))
         w_ref[...] = a_ref[...] + fold(dot_nn(energy, image_t[...]))
@@ -565,7 +637,8 @@
         def _():
             image = fold(dot_nn(split, pick[...]))
             tr_w[...] = image
-            send_faces(step, 1, image)
+            store_faces(1, image)
+            start_faces(step, 1)
 
         gather_middle(step + 1)
 
@@ -632,7 +705,10 @@
             vmem((NB * TPR * TILE, TILE), F32),
             vmem((NB * TPR * TILE, TILE), F32),
             vmem((DEFL, M), F32),
-            vmem((GRID, DEFL, KROW), F32),
+            vmem((DEFL, GRID * KROW), F32),
+            vmem((GRID, 2, DEFL, 128), F32),
+            vmem((8, DEFL, KROW), F32),
+            vmem((8, DEFL, KROW), F32),
             vmem((4, FACE), jnp.int32),
             vmem((NB, TPR * TILE, 2 * TILE), BF16),
             vmem((NB, TPR * TILE, 2 * TILE), BF16),
@@ -641,8 +717,10 @@
             vmem((128, M), BF16),
             vmem((2 * DEFL, M), BF16),
             vmem((128, SLOTS), BF16),
-            vmem((KROW, KROW), BF16),
-            vmem((KROW, KROW), BF16),
+            vmem((KROW, KROW // 2), BF16),
+            vmem((KROW, KROW // 2), BF16),
+            vmem((KROW // 2, KROW), BF16),
+            vmem((KROW // 2, KROW), BF16),
             vmem((M, SLOTS), BF16),
             vmem((256, 128), BF16),
             vmem((NB, wide, TILE), BF16),
@@ -668,6 +746,8 @@
             dma,
             dma,
             dma,
+            dma,
+            dma,
             dma((ITERS + 1,)),
             dma,
             dma((ITERS + 1,)),

time: 67.8 us -> 64.4 us (0.950)
  Pallas kernels: 67 us -> 63.7 us
    pallas_call x1, Pallas kernels: 65.4 us -> 62.1 us  [shards(): pl.pallas_call(kernel, out_shape=(field, field, field), in_specs=[anywher...]
where the time goes in v4:
time: 64.4 us; the launch traced here: 64.3 us
  Pallas kernels  63.7 us (99%)
    pallas_call x1, Pallas kernels, shards(): pl.pallas_call(kernel, out_shape=(field, field, field), in_specs=[anywher...  62.1 us
    pallas_call x1, Pallas kernels, shards(): pl.pallas_call(publish, out_shape=(field, field, field), in_specs=[vector...  1.58 us

profile of v4, /device:TPU:1, one launch (start us, length us, event | category | flops | bytes accessed | tf_op | source)
XLA Modules:
  0.0 64.3 jit_solution(1470208656682552751)
XLA Ops:
  0.6 62.1 %feti.1 = (f32[8,2048]{1,0:T(8,128)}, f32[8,2048]{1,0:T(8,128)}, f32[8,2048]{1,0:T(8,128)}) custom-call(f32[8,2048]{1,0:T(8,128)} %rhs.1, f32[8192,128]{1,0:T(8,128)} %flex.1, s32[4,16]{1,0:T(4,128)} %bitcast.2, f32[8192,128]{1,0:T(8,128)} %stiff.1, s32[4,16]{1,0:T(4,128)} %bitcast.3, f32[32,2048]{1,0:T(8,128)} %defl.1, f32[32,8192]{1,0:T(8,128)} %coarse.1, ...), custom_call_target="tpu_custom_call" | custom-call | tf_op jit(solution)/shard_map/feti/pallas_call | solution.py:697
  62.7 1.6 %publish.1 = (f32[8,2048]{1,0:T(8,128)}, f32[8,2048]{1,0:T(8,128)}, f32[8,2048]{1,0:T(8,128)}) custom-call(f32[8,2048]{1,0:T(8,128)} %get-tuple-element.6.x_in, f32[8,2048]{1,0:T(8,128)} %get-tuple-element.7.r_in, f32[8,2048]{1,0:T(8,128)} %get-tuple-element.8.z_in), custom_call_target="tpu_custom_call" | custom-call | tf_op jit(solution)/shard_map/publish/pallas_call | solution.py:764

commit v5 on v4

--- a/solution.py
+++ b/solution.py
@@ -291,12 +291,6 @@
     defl_t[2 * DEFL :] = jnp.zeros((128 - 2 * DEFL, M), BF16)
     started = coefficients_of(dot_nt(parts(r_ref[...]), defl_t[...]))
     c_ref[...] = pltpu.roll(started, DEFL, 1)
-    pl.semaphore_wait(barrier, 2 * (GRID - 1))
-    for there in row_partners:
-        for part in range(2):
-            coarse_copy(there, part).start()
-    gather_start(0, turn(started, place), jnp.zeros((LOADS, 128), F32), ())
-
     load_coarse.wait()
     group32 = lane_ids((DEFL, 128)) // DEFL
     after, ahead = (pair + 1) % 4, (pair + 3) % 4
@@ -312,11 +306,17 @@
                     value = pltpu.roll(value, shift, 1)
                 packed = value if packed is None else jnp.where(group32 == offset, value, packed)
             across_out[piece, :, quarter * 128 : (quarter + 1) * 128] = packed
+    pl.semaphore_wait(barrier, 2 * (GRID - 1))
     for piece, there in ((4, after * 4), (5, after * 4 + 1), (6, ahead * 4 + 2), (7, ahead * 4 + 3)):
         across_copy(piece, there, 4 + place).start()
     for step in range(1, 4):
         other = (place + step) % 4
         across_copy(other, pair * 4 + other, place).start()
+    for there in row_partners:
+        for part in range(2):
+            coarse_copy(there, part).start()
+    gather_start(0, turn(started, place), jnp.zeros((LOADS, 128), F32), ())
+
     across_in[place] = across_out[place]
     for part in range(2):
         coarse_f[i, part] = coarse_own[:, coarse_lanes(i, far_groups[part])]
@@ -496,7 +496,8 @@
     for block in range(NB):
         span = slice(block * TILE, (block + 1) * TILE)
         a_ref[:, span] = r_ref[:, span] + applied[block][0:LOADS]
-        image_t[:, span] = parts(defl_f[:, span] + applied[block][LOADS:wide])
+        image_t[0 : 2 * DEFL, span] = parts(defl_f[:, span] + applied[block][LOADS:wide])
+    image_t[2 * DEFL :] = jnp.zeros((128 - 2 * DEFL, M), BF16)
 
     for face, (inside, device, slot) in enumerate(sides):
 
@@ -534,7 +535,7 @@
     def against(value):
         return jnp.concatenate([parts(value), jnp.zeros((2 * DEFL, FACE), BF16)], axis=0)
 
-    own = dot_nt(image_t[...], defl_t[...])
+    own = dot_nt(image_t[0 : 2 * DEFL], defl_t[...])
     for face in range(4):
         own = own + dot_nt(parts(masked[face]), trace_t[:, face * FACE : (face + 1) * FACE])
     north = paired(dot_nt(parts(others[0]), trace_t[:, 0:FACE]))
@@ -625,7 +626,7 @@
         start_faces(step, 0)
         x_ref[...] = x_ref[...] + alpha * p
         z_ref[...] = r_ref[...] + fold(dot_nn(energy, defl_t[0 : 2 * DEFL]))
-        w_ref[...] = a_ref[...] + fold(dot_nn(energy, image_t[...]))
+        w_ref[...] = a_ref[...] + fold(dot_nn(energy, image_t[0 : 2 * DEFL]))
         jump = take_faces(step, 0, traces)
         w = w_ref[...] + fold(dot_nt(parts(jump), pick[...]))
         w_ref[...] = w
@@ -649,14 +650,15 @@
             middle = backward(blocks_a, stiff_t, stiff_s, spread)
             for block in range(NB):
                 blocks_b[block] = parts(middle[block])
-            local = backward(blocks_b, flex_t, flex_s, spread)
-            image = w_ref[...] + jnp.concatenate(local, axis=1)
-            bw_ref[...] = image
             jump = take_faces(step, 1, tr_w[...])
             jump_w[...] = jump
-            found = operator_coefficients(image, jump)
+            found = coefficients_of(
+                dot_nt(split, image_t[...]) + dot_nt(parts(jump), trace_t[...])
+            )
             gw_ref[0] = turn(found, place)
             gw_ref[1] = pltpu.roll(found, DEFL, 1)
+            local = backward(blocks_b, flex_t, flex_s, spread)
+            bw_ref[...] = w_ref[...] + jnp.concatenate(local, axis=1)
 
         gathered = gather_end(step + 1)
 
@@ -715,7 +717,7 @@
             vmem((NB * LOADS, NB * TPR * LOADS), BF16),
             vmem((NB * LOADS, NB * TPR * LOADS), BF16),
             vmem((128, M), BF16),
-            vmem((2 * DEFL, M), BF16),
+            vmem((128, M), BF16),
             vmem((128, SLOTS), BF16),
             vmem((KROW, KROW // 2), BF16),
             vmem((KROW, KROW // 2), BF16),

time: 64.4 us -> 65 us (level)
  no operation moved by 1% of the time
where the time goes in v5:
time: 65 us; the launch traced here: 64.8 us
  Pallas kernels  64.2 us (99%)
    pallas_call x1, Pallas kernels, shards(): pl.pallas_call(kernel, out_shape=(field, field, field), in_specs=[anywher...  62.6 us
    pallas_call x1, Pallas kernels, shards(): pl.pallas_call(publish, out_shape=(field, field, field), in_specs=[vector...  1.58 us

profile of v5, /device:TPU:1, one launch (start us, length us, event | category | flops | bytes accessed | tf_op | source)
XLA Modules:
  0.0 64.8 jit_solution(4414212918200619046)
XLA Ops:
  0.6 62.6 %feti.1 = (f32[8,2048]{1,0:T(8,128)}, f32[8,2048]{1,0:T(8,128)}, f32[8,2048]{1,0:T(8,128)}) custom-call(f32[8,2048]{1,0:T(8,128)} %rhs.1, f32[8192,128]{1,0:T(8,128)} %flex.1, s32[4,16]{1,0:T(4,128)} %bitcast.2, f32[8192,128]{1,0:T(8,128)} %stiff.1, s32[4,16]{1,0:T(4,128)} %bitcast.3, f32[32,2048]{1,0:T(8,128)} %defl.1, f32[32,8192]{1,0:T(8,128)} %coarse.1, ...), custom_call_target="tpu_custom_call" | custom-call | tf_op jit(solution)/shard_map/feti/pallas_call | solution.py:699
  63.2 1.6 %publish.1 = (f32[8,2048]{1,0:T(8,128)}, f32[8,2048]{1,0:T(8,128)}, f32[8,2048]{1,0:T(8,128)}) custom-call(f32[8,2048]{1,0:T(8,128)} %get-tuple-element.6.x_in, f32[8,2048]{1,0:T(8,128)} %get-tuple-element.7.r_in, f32[8,2048]{1,0:T(8,128)} %get-tuple-element.8.z_in), custom_call_target="tpu_custom_call" | custom-call | tf_op jit(solution)/shard_map/publish/pallas_call | solution.py:766

commit v6 on v5

--- a/solution.py
+++ b/solution.py
@@ -291,6 +291,12 @@
     defl_t[2 * DEFL :] = jnp.zeros((128 - 2 * DEFL, M), BF16)
     started = coefficients_of(dot_nt(parts(r_ref[...]), defl_t[...]))
     c_ref[...] = pltpu.roll(started, DEFL, 1)
+    pl.semaphore_wait(barrier, 2 * (GRID - 1))
+    for there in row_partners:
+        for part in range(2):
+            coarse_copy(there, part).start()
+    gather_start(0, turn(started, place), jnp.zeros((LOADS, 128), F32), ())
+
     load_coarse.wait()
     group32 = lane_ids((DEFL, 128)) // DEFL
     after, ahead = (pair + 1) % 4, (pair + 3) % 4
@@ -306,17 +312,11 @@
                     value = pltpu.roll(value, shift, 1)
                 packed = value if packed is None else jnp.where(group32 == offset, value, packed)
             across_out[piece, :, quarter * 128 : (quarter + 1) * 128] = packed
-    pl.semaphore_wait(barrier, 2 * (GRID - 1))
     for piece, there in ((4, after * 4), (5, after * 4 + 1), (6, ahead * 4 + 2), (7, ahead * 4 + 3)):
         across_copy(piece, there, 4 + place).start()
     for step in range(1, 4):
         other = (place + step) % 4
         across_copy(other, pair * 4 + other, place).start()
-    for there in row_partners:
-        for part in range(2):
-            coarse_copy(there, part).start()
-    gather_start(0, turn(started, place), jnp.zeros((LOADS, 128), F32), ())
-
     across_in[place] = across_out[place]
     for part in range(2):
         coarse_f[i, part] = coarse_own[:, coarse_lanes(i, far_groups[part])]
@@ -576,9 +576,12 @@
         energy = jnp.where(group8 == 1, e_r[...], 0.0)
         return parts(energy + pltpu.roll(energy, 128 - DEFL, 1))[:, 0 : 2 * DEFL]
 
+    def across(ref, width):
+        return jnp.concatenate([ref[...]] * (width // 128), axis=1)
+
     def advance():
-        alpha = alpha_ref[:, 0:1]
-        beta = beta_ref[:, 0:1]
+        alpha = across(alpha_ref, M)
+        beta = across(beta_ref, M)
         direction = z_ref[...] + beta * p_ref[...]
         image = w_ref[...] + beta * q_ref[...]
         p_ref[...] = direction
@@ -597,20 +600,22 @@
         a = a_ref[...] - alpha * applied
         a_ref[...] = a
         for layout in range(2):
-            image = gw_ref[layout] + beta * gq_ref[layout]
+            image = gw_ref[layout] + beta_ref[...] * gq_ref[layout]
             gq_ref[layout] = image
-            gr_ref[layout] = gr_ref[layout] - alpha * image
-        image = own_ref[...] + beta * cq_ref[...]
+            gr_ref[layout] = gr_ref[layout] - alpha_ref[...] * image
+        image = own_ref[...] + beta_ref[...] * cq_ref[...]
         cq_ref[...] = image
-        c = c_ref[...] - alpha * image
+        c = c_ref[...] - alpha_ref[...] * image
         c_ref[...] = c
-        trace_q = tr_w[...] + beta * tr_q[...]
+        alpha_s = across(alpha_ref, SLOTS)
+        beta_s = across(beta_ref, SLOTS)
+        trace_q = tr_w[...] + beta_s * tr_q[...]
         tr_q[...] = trace_q
-        tr = tr_r[...] - alpha * trace_q
+        tr = tr_r[...] - alpha_s * trace_q
         tr_r[...] = tr
-        jump_q_now = jump_w[...] + beta * jump_q[...]
+        jump_q_now = jump_w[...] + beta_s * jump_q[...]
         jump_q[...] = jump_q_now
-        jump_now = jump_r[...] - alpha * jump_q_now
+        jump_now = jump_r[...] - alpha_s * jump_q_now
         jump_r[...] = jump_now
         sum_zar = row_sum(r * a) + row_sum(tr * jump_now) + row_sum(energies * gr_ref[1])
         sum_rz = row_sum(r * r) + row_sum(energies * c)
@@ -662,15 +667,18 @@
 
         gathered = gather_end(step + 1)
 
-        def total(index):
-            return gathered[:, 3 * DEFL + index : 3 * DEFL + index + 1]
-
-        new_beta = -total(3) / s1_ref[:, 0:1]
-        curvature = total(0) + new_beta * total(3)
-        new_alpha = (total(1) + new_beta * total(2)) / curvature
-        s1_ref[...] = jnp.broadcast_to(curvature, (LOADS, 128))
-        alpha_ref[...] = jnp.broadcast_to(new_alpha, (LOADS, 128))
-        beta_ref[...] = jnp.broadcast_to(new_beta, (LOADS, 128))
+        sum_zw, sum_rz, sum_rp, sum_zq = [
+            jnp.broadcast_to(
+                gathered[:, 3 * DEFL + index : 3 * DEFL + index + 1], (LOADS, 128)
+            )
+            for index in range(4)
+        ]
+        new_beta = -sum_zq / s1_ref[...]
+        curvature = sum_zw + new_beta * sum_zq
+        new_alpha = (sum_rz + new_beta * sum_rp) / curvature
+        s1_ref[...] = curvature
+        alpha_ref[...] = new_alpha
+        beta_ref[...] = new_beta
         energy_q = jnp.where(group8 < 3, gathered, 0.0) + new_beta * e_q[...]
         e_q[...] = energy_q
         e_r[...] = e_r[...] - new_alpha * energy_q

time: 65 us -> 63.2 us (0.972)
  Pallas kernels: 64.2 us -> 62.4 us
    pallas_call x1, Pallas kernels: 62.6 us -> 60.9 us  [shards(): pl.pallas_call(kernel, out_shape=(field, field, field), in_specs=[anywher...]
where the time goes in v6:
time: 63.2 us; the launch traced here: 63.1 us
  Pallas kernels  62.4 us (99%)
  between operations  0.64 us (1%)
    pallas_call x1, Pallas kernels, shards(): pl.pallas_call(kernel, out_shape=(field, field, field), in_specs=[anywher...  60.9 us
    pallas_call x1, Pallas kernels, shards(): pl.pallas_call(publish, out_shape=(field, field, field), in_specs=[vector...  1.58 us

profile of v6, /device:TPU:1, one launch (start us, length us, event | category | flops | bytes accessed | tf_op | source)
XLA Modules:
  0.0 63.1 jit_solution(11857783051512748937)
XLA Ops:
  0.6 60.9 %feti.1 = (f32[8,2048]{1,0:T(8,128)}, f32[8,2048]{1,0:T(8,128)}, f32[8,2048]{1,0:T(8,128)}) custom-call(f32[8,2048]{1,0:T(8,128)} %rhs.1, f32[8192,128]{1,0:T(8,128)} %flex.1, s32[4,16]{1,0:T(4,128)} %bitcast.2, f32[8192,128]{1,0:T(8,128)} %stiff.1, s32[4,16]{1,0:T(4,128)} %bitcast.3, f32[32,2048]{1,0:T(8,128)} %defl.1, f32[32,8192]{1,0:T(8,128)} %coarse.1, ...), custom_call_target="tpu_custom_call" | custom-call | tf_op jit(solution)/shard_map/feti/pallas_call | solution.py:707
  61.5 1.6 %publish.1 = (f32[8,2048]{1,0:T(8,128)}, f32[8,2048]{1,0:T(8,128)}, f32[8,2048]{1,0:T(8,128)}) custom-call(f32[8,2048]{1,0:T(8,128)} %get-tuple-element.6.x_in, f32[8,2048]{1,0:T(8,128)} %get-tuple-element.7.r_in, f32[8,2048]{1,0:T(8,128)} %get-tuple-element.8.z_in), custom_call_target="tpu_custom_call" | custom-call | tf_op jit(solution)/shard_map/publish/pallas_call | solution.py:774

commit v7 on v6

--- a/solution.py
+++ b/solution.py
@@ -624,11 +624,11 @@
         energy = energy_parts()
         traces = tr + fold(dot_nn(energy, trace_t[0 : 2 * DEFL]))
         store_faces(0, traces)
+        start_faces(step, 0)
         gather_start(
             step + 1, coefficients + gr_ref[0], energies, (sum_zar, sum_rz, sum_rp, sum_zq)
         )
 
-        start_faces(step, 0)
         x_ref[...] = x_ref[...] + alpha * p
         z_ref[...] = r_ref[...] + fold(dot_nn(energy, defl_t[0 : 2 * DEFL]))
         w_ref[...] = a_ref[...] + fold(dot_nn(energy, image_t[0 : 2 * DEFL]))

time: 63.2 us -> 61.9 us (0.979)
  Pallas kernels: 62.4 us -> 61.1 us
    pallas_call x1, Pallas kernels: 60.9 us -> 59.5 us  [shards(): pl.pallas_call(kernel, out_shape=(field, field, field), in_specs=[anywher...]
where the time goes in v7:
time: 61.9 us; the launch traced here: 61.8 us
  Pallas kernels  61.1 us (99%)
  between operations  0.64 us (1%)
    pallas_call x1, Pallas kernels, shards(): pl.pallas_call(kernel, out_shape=(field, field, field), in_specs=[anywher...  59.5 us
    pallas_call x1, Pallas kernels, shards(): pl.pallas_call(publish, out_shape=(field, field, field), in_specs=[vector...  1.58 us

profile of v7, /device:TPU:1, one launch (start us, length us, event | category | flops | bytes accessed | tf_op | source)
XLA Modules:
  0.0 61.8 jit_solution(818869434689473439)
XLA Ops:
  0.6 59.5 %feti.1 = (f32[8,2048]{1,0:T(8,128)}, f32[8,2048]{1,0:T(8,128)}, f32[8,2048]{1,0:T(8,128)}) custom-call(f32[8,2048]{1,0:T(8,128)} %rhs.1, f32[8192,128]{1,0:T(8,128)} %flex.1, s32[4,16]{1,0:T(4,128)} %bitcast.2, f32[8192,128]{1,0:T(8,128)} %stiff.1, s32[4,16]{1,0:T(4,128)} %bitcast.3, f32[32,2048]{1,0:T(8,128)} %defl.1, f32[32,8192]{1,0:T(8,128)} %coarse.1, ...), custom_call_target="tpu_custom_call" | custom-call | tf_op jit(solution)/shard_map/feti/pallas_call | solution.py:707
  60.2 1.6 %publish.1 = (f32[8,2048]{1,0:T(8,128)}, f32[8,2048]{1,0:T(8,128)}, f32[8,2048]{1,0:T(8,128)}) custom-call(f32[8,2048]{1,0:T(8,128)} %get-tuple-element.6.x_in, f32[8,2048]{1,0:T(8,128)} %get-tuple-element.7.r_in, f32[8,2048]{1,0:T(8,128)} %get-tuple-element.8.z_in), custom_call_target="tpu_custom_call" | custom-call | tf_op jit(solution)/shard_map/publish/pallas_call | solution.py:774
